TPU v7x, 32 devices: a whole 2x2x4 slice. The times are simulated.
32 devices in a mesh: dp: 8 (over z, x), shard: 4 (over y, core).
Axes of the slice: x: 2, y: 2, z: 4, core: 2. Of those that a mesh axis runs over, the one named last changes fastest.
Arguments:
- noisy: float32 [128, 256, 16], P(('dp', 'shard')), may hold values from -6 to 6
- velocity: float32 [128, 256, 16], P(('dp', 'shard')), may hold values from -6 to 6
- tstep_idx: int32 [128], P(('dp', 'shard')), may hold values from 0 to 999
- class_ids: int32 [128], P(('dp', 'shard')), may hold values from 0 to 1000
- time_weight: float32 [128], P(('dp', 'shard')), may hold values from 0.3 to 3
- dino: bfloat16 [128, 256, 768], P(('dp', 'shard')), may hold values from -6 to 6
- owner_map: int32 [12], replicated, may hold values from 0 to 11, each once
- adam_flat: float32 [2129920], P(('dp', 'shard')), may hold values from -4 to 4
- adam_m: float32 [2129920], P(('dp', 'shard')), may hold values from -0.015625 to 0.015625
- adam_v: float32 [2129920], P(('dp', 'shard')), may hold values from 1e-06 to 0.0001
- blocks_w: float32 [12, 384, 384], P('shard'), may hold values from -0.3125 to 0.3125
- stat_left: float32 [12, 384, 384], P('shard'), may hold values from -0.005 to 0.01, as said below
- stat_right: float32 [12, 384, 384], P('shard'), may hold values from -0.005 to 0.01, as said below
- root_left: float32 [12, 384, 384], P('shard'), may hold values from -3 to 3, as said below
- root_right: float32 [12, 384, 384], P('shard'), may hold values from -3 to 3, as said below
Outputs:
- loss: float32 [], replicated
- block_update: float32 [12, 384, 384], P('shard')
- stat_left_new: float32 [12, 384, 384], P('shard')
- stat_right_new: float32 [12, 384, 384], P('shard')
- adam_update: float32 [2129920], P(('dp', 'shard'))
- adam_m_new: float32 [2129920], P(('dp', 'shard'))
- adam_v_new: float32 [2129920], P(('dp', 'shard'))
Inputs may be any that keep to these rules, and one draw needn't show every extreme that they name: `owner_map`: each block number appears once. `stat_left`: each slot is symmetric positive definite. `stat_right`: each slot is symmetric positive definite. `root_left`: each slot is symmetric positive definite. `root_right`: each slot is symmetric positive definite.
All inputs are finite; a program needn't handle non-finite values.
Results may differ from a plain program's by a relative error of at most 0.0097.
Values may be sent and summed in bfloat16 or wider, within the bound.
No kernel may reach another device: no remote copies, remote signals or barrier semaphores. Data moves between devices by JAX's collectives and lax.ppermute only.
A program may use at most 192 MiB of HBM per device.

v0:
```python
import functools
import math

import jax
import jax.numpy as jnp
from jax import lax
from jax.sharding import PartitionSpec as P

D = 384
HEADS = 6
HDIM = 64
F = 1536
PD = 16
GRID = 16
SEQ = 256
FREQ = 256
NCLS = 1001
DINO = 768
STEP = 10
NBLK = 12
ADAM_LEN = 2125072
ADAM_PAD = 2129920


HIGHEST = lax.Precision.HIGHEST
BETA_ONE = 0.9
BETA_TWO = 0.95
ADAM_EPS = 1e-08
ADAM_RATE = 0.01
DECAY_RATE = 0.1
STAT_BETA = 0.9
SHAMPOO_RATE = 0.02
RMS_EPS = 1e-08
REPA_WEIGHT = 0.5
NORM_EPS = 1e-06


def segment_shapes():
    return [
        (PD, D),
        (D,),
        (FREQ, D),
        (D,),
        (D, D),
        (D,),
        (NCLS, D),
        (D, 6 * D),
        (6 * D,),
        (D,),
        (D,),
        (D,),
        (F,),
        (D,),
        (D, 2 * D),
        (2 * D,),
        (D, PD),
        (PD,),
        (D, DINO),
        (DINO,),
    ]


def unflatten(flat):
    pieces = []
    offset = 0
    for seg_dims in segment_shapes():
        length = math.prod(seg_dims)
        pieces.append(flat[offset : offset + length].reshape(seg_dims))
        offset += length
    return pieces


def position_table():
    quarter = D // 4
    frequencies = 1.0 / 10000.0 ** (jnp.arange(quarter, dtype=jnp.float32) / quarter)
    cell_ids = jnp.arange(SEQ, dtype=jnp.int32)
    row_arg = (cell_ids // GRID).astype(jnp.float32)[:, None] * frequencies[None, :]
    col_arg = (cell_ids % GRID).astype(jnp.float32)[:, None] * frequencies[None, :]
    return jnp.concatenate(
        [jnp.sin(col_arg), jnp.cos(col_arg), jnp.sin(row_arg), jnp.cos(row_arg)], axis=1
    )


def time_features(tstep_idx):
    half_freq = FREQ // 2
    frequencies = jnp.exp(-math.log(10000.0) * jnp.arange(half_freq, dtype=jnp.float32) / half_freq)
    angles = (tstep_idx.astype(jnp.float32) + 0.5)[:, None] * frequencies[None, :]
    return jnp.concatenate([jnp.cos(angles), jnp.sin(angles)], axis=1)


def normalize(values):
    centered = values - jnp.mean(values, axis=-1, keepdims=True)
    inv_dev = lax.rsqrt(jnp.mean(centered * centered, axis=-1, keepdims=True) + NORM_EPS)
    return (centered * inv_dev, inv_dev)


def normalize_back(grad_in, normed, inv_dev):
    return inv_dev * (
        grad_in
        - jnp.mean(grad_in, axis=-1, keepdims=True)
        - normed * jnp.mean(grad_in * normed, axis=-1, keepdims=True)
    )


def condition_terms(
    tstep_idx,
    class_ids,
    time_in_weight,
    time_in_bias,
    time_out_weight,
    time_out_bias,
    class_table,
    mod_weight,
    mod_bias,
    final_mod_weight,
    final_mod_bias,
):
    features = time_features(tstep_idx)
    time_hidden = jax.nn.silu(jnp.dot(features, time_in_weight, precision=HIGHEST) + time_in_bias)
    onehot_class = (class_ids[:, None] == jnp.arange(NCLS, dtype=jnp.int32)[None, :]).astype(
        jnp.float32
    )
    condition = (
        jnp.dot(time_hidden, time_out_weight, precision=HIGHEST)
        + time_out_bias
        + jnp.dot(onehot_class, class_table, precision=HIGHEST)
    )
    cond_act = jax.nn.silu(condition)
    modulation = jnp.dot(cond_act, mod_weight, precision=HIGHEST) + mod_bias
    final_mods = jnp.dot(cond_act, final_mod_weight, precision=HIGHEST) + final_mod_bias
    return (modulation, final_mods)


def cosine_total(aligned, dino_f):
    products = jnp.sum(aligned * dino_f, axis=-1)
    return jnp.sum(
        products
        * lax.rsqrt(jnp.sum(aligned * aligned, axis=-1) + NORM_EPS)
        * lax.rsqrt(jnp.sum(dino_f * dino_f, axis=-1) + NORM_EPS)
    )


def matmul(left, right):
    return jnp.dot(left, right, preferred_element_type=jnp.float32)


def row_total(rounded):
    return jnp.sum(rounded.astype(jnp.float32), axis=0)


def body(
    noisy,
    velocity,
    tstep_idx,
    class_ids,
    time_weight,
    dino,
    owner_map,
    adam_flat,
    adam_m,
    adam_v,
    blocks_w,
    stat_left,
    stat_right,
    root_left,
    root_right,
):
    devices = lax.axis_size("dp") * lax.axis_size("shard")
    images = noisy.shape[0]
    seq = noisy.shape[1]
    total_img = images * devices
    rows = images * seq
    fc_ratio = F // D
    flat_low = lax.all_gather(adam_flat.astype(jnp.bfloat16), ("dp", "shard"), axis=0, tiled=True)
    slot_low = lax.all_gather(blocks_w.astype(jnp.bfloat16), "shard", axis=0, tiled=True)
    block_ids = jnp.arange(NBLK, dtype=jnp.int32)
    slot_of = jnp.sum(
        block_ids[:, None] * (owner_map[:, None] == block_ids[None, :]).astype(jnp.int32), axis=0
    )
    blocks = jnp.take(slot_low, slot_of, axis=0)
    w_qkv = jnp.concatenate([blocks[0], blocks[1], blocks[2]], axis=1)
    w_proj = blocks[3]
    w_up = jnp.concatenate([blocks[4 + which] for which in range(fc_ratio)], axis=1)
    w_down = blocks[4 + fc_ratio :].reshape(F, D)
    pieces_low = unflatten(flat_low)
    pieces = [piece.astype(jnp.float32) for piece in pieces_low]
    (
        patch_weight,
        patch_bias,
        time_in_weight,
        time_in_bias,
        time_out_weight,
        time_out_bias,
        class_table,
        mod_weight,
        mod_bias,
        query_bias,
        value_bias,
        proj_bias,
        hidden_bias,
        down_bias,
        final_mod_weight,
        final_mod_bias,
        final_weight,
        final_bias,
        align_weight,
        align_bias,
    ) = pieces
    patch_low = pieces_low[0]
    final_low = pieces_low[16]
    align_low = pieces_low[18]
    cond_weights = (
        time_in_weight,
        time_in_bias,
        time_out_weight,
        time_out_bias,
        class_table,
        mod_weight,
        mod_bias,
        final_mod_weight,
        final_mod_bias,
    )
    (modulation, final_mods), cond_back = jax.vjp(
        functools.partial(condition_terms, tstep_idx, class_ids), *cond_weights
    )
    shift_one, scale_one, gate_one, shift_two, scale_two, gate_two = [
        modulation[:, None, which * D : (which + 1) * D] for which in range(6)
    ]
    final_shift = final_mods[:, None, :D]
    final_scale = final_mods[:, None, D:]
    noisy_low = noisy.astype(jnp.bfloat16).reshape(rows, PD)
    hidden0 = (matmul(noisy_low, patch_low) + patch_bias).reshape(images, seq, D) + position_table()
    norm_one, inv_one = normalize(hidden0)
    act_one = (norm_one * (1.0 + scale_one) + shift_one).astype(jnp.bfloat16).reshape(rows, D)
    qkv_bias = jnp.concatenate([query_bias, jnp.zeros((D,), jnp.float32), value_bias])
    projected = (
        (matmul(act_one, w_qkv) + qkv_bias)
        .astype(jnp.bfloat16)
        .reshape(images, seq, 3, HEADS, HDIM)
    )
    queries = projected[:, :, 0]
    key_part = projected[:, :, 1]
    values = projected[:, :, 2]
    scale_qk = HDIM ** (-0.5)
    scores = (
        jnp.einsum("gqhe,gkhe->ghqk", queries, key_part, preferred_element_type=jnp.float32)
        * scale_qk
    )
    row_max = jnp.max(scores, axis=-1, keepdims=True)
    log_total = row_max + jnp.log(jnp.sum(jnp.exp(scores - row_max), axis=-1, keepdims=True))
    probs_low = jnp.exp(scores - log_total).astype(jnp.bfloat16)
    attended = (
        jnp.einsum("ghqk,gkhe->gqhe", probs_low, values, preferred_element_type=jnp.float32)
        .reshape(rows, D)
        .astype(jnp.bfloat16)
    )
    branch_one = (matmul(attended, w_proj) + proj_bias).reshape(images, seq, D)
    hidden1 = hidden0 + gate_one * branch_one
    norm_two, inv_two = normalize(hidden1)
    act_two = (norm_two * (1.0 + scale_two) + shift_two).astype(jnp.bfloat16).reshape(rows, D)
    inner_pre = matmul(act_two, w_up) + hidden_bias
    gelu_out, gelu_back = jax.vjp(functools.partial(jax.nn.gelu, approximate=True), inner_pre)
    gelu_low = gelu_out.astype(jnp.bfloat16)
    branch_two = (matmul(gelu_low, w_down) + down_bias).reshape(images, seq, D)
    hidden2 = hidden1 + gate_two * branch_two
    norm_three, inv_three = normalize(hidden2)
    act_three = (
        (norm_three * (1.0 + final_scale) + final_shift).astype(jnp.bfloat16).reshape(rows, D)
    )
    output = (matmul(act_three, final_low) + final_bias).reshape(images, seq, PD)
    errors = output - velocity
    main_term = jnp.sum(time_weight[:, None, None] * errors * errors) / (total_img * SEQ * PD)
    hidden1_low = hidden1.astype(jnp.bfloat16).reshape(rows, D)
    aligned = matmul(hidden1_low, align_low) + align_bias
    dino_f = dino.astype(jnp.float32).reshape(rows, DINO)
    cosine_sum, cosine_back = jax.vjp(functools.partial(cosine_total, dino_f=dino_f), aligned)
    align_scale = REPA_WEIGHT / (total_img * SEQ)
    loss_local = main_term - align_scale * cosine_sum
    back_output = (
        (2.0 * time_weight[:, None, None] * errors / (total_img * SEQ * PD))
        .reshape(rows, PD)
        .astype(jnp.bfloat16)
    )
    grad_final = matmul(act_three.T, back_output)
    grad_final_bias = row_total(back_output)
    back_three = matmul(back_output, final_low.T).reshape(images, seq, D)
    grad_final_shift = jnp.sum(back_three, axis=1)
    grad_final_scale = jnp.sum(back_three * norm_three, axis=1)
    back_hidden2 = normalize_back(back_three * (1.0 + final_scale), norm_three, inv_three)
    back_branch_two = (back_hidden2 * gate_two).reshape(rows, D).astype(jnp.bfloat16)
    grad_gate_two = jnp.sum(back_hidden2 * branch_two, axis=1)
    grad_down = matmul(gelu_low.T, back_branch_two)
    grad_down_bias = row_total(back_branch_two)
    back_inner = gelu_back(matmul(back_branch_two, w_down.T))[0].astype(jnp.bfloat16)
    grad_up = matmul(act_two.T, back_inner)
    grad_hidden_bias = row_total(back_inner)
    back_two = matmul(back_inner, w_up.T).reshape(images, seq, D)
    grad_shift_two = jnp.sum(back_two, axis=1)
    grad_scale_two = jnp.sum(back_two * norm_two, axis=1)
    back_aligned = cosine_back(jnp.asarray(-align_scale, jnp.float32))[0].astype(jnp.bfloat16)
    grad_align = matmul(hidden1_low.T, back_aligned)
    grad_align_bias = row_total(back_aligned)
    back_hidden1 = (
        back_hidden2
        + normalize_back(back_two * (1.0 + scale_two), norm_two, inv_two)
        + matmul(back_aligned, align_low.T).reshape(images, seq, D)
    )
    back_branch_one = (back_hidden1 * gate_one).reshape(rows, D).astype(jnp.bfloat16)
    grad_gate_one = jnp.sum(back_hidden1 * branch_one, axis=1)
    grad_proj = matmul(attended.T, back_branch_one)
    grad_proj_bias = row_total(back_branch_one)
    back_attended = (
        matmul(back_branch_one, w_proj.T).astype(jnp.bfloat16).reshape(images, seq, HEADS, HDIM)
    )
    back_probs = jnp.einsum(
        "gqhe,gkhe->ghqk", back_attended, values, preferred_element_type=jnp.float32
    )
    grad_values = jnp.einsum(
        "ghqk,gqhe->gkhe", probs_low, back_attended, preferred_element_type=jnp.float32
    )
    scores_again = (
        jnp.einsum("gqhe,gkhe->ghqk", queries, key_part, preferred_element_type=jnp.float32)
        * scale_qk
    )
    probs_again = jnp.exp(scores_again - log_total)
    back_scores = (
        probs_again * (back_probs - jnp.sum(back_probs * probs_again, axis=-1, keepdims=True))
    ).astype(jnp.bfloat16)
    grad_queries = (
        jnp.einsum("ghqk,gkhe->gqhe", back_scores, key_part, preferred_element_type=jnp.float32)
        * scale_qk
    )
    grad_keys = (
        jnp.einsum("ghqk,gqhe->gkhe", back_scores, queries, preferred_element_type=jnp.float32)
        * scale_qk
    )
    back_projected = (
        jnp.stack([grad_queries, grad_keys, grad_values], axis=2)
        .reshape(rows, 3 * D)
        .astype(jnp.bfloat16)
    )
    grad_qkv = matmul(act_one.T, back_projected)
    grad_qkv_bias = row_total(back_projected)
    back_one = matmul(back_projected, w_qkv.T).reshape(images, seq, D)
    grad_shift_one = jnp.sum(back_one, axis=1)
    grad_scale_one = jnp.sum(back_one * norm_one, axis=1)
    back_hidden0 = (
        (back_hidden1 + normalize_back(back_one * (1.0 + scale_one), norm_one, inv_one))
        .reshape(rows, D)
        .astype(jnp.bfloat16)
    )
    grad_patch = matmul(noisy_low.T, back_hidden0)
    grad_patch_bias = row_total(back_hidden0)
    grad_modulation = jnp.concatenate(
        [
            grad_shift_one,
            grad_scale_one,
            grad_gate_one,
            grad_shift_two,
            grad_scale_two,
            grad_gate_two,
        ],
        axis=1,
    )
    grad_final_mods = jnp.concatenate([grad_final_shift, grad_final_scale], axis=1)
    cond_grads = cond_back((grad_modulation, grad_final_mods))
    grad_list = (
        [grad_patch, grad_patch_bias]
        + list(cond_grads[:7])
        + [
            grad_qkv_bias[:D],
            grad_qkv_bias[2 * D :],
            grad_proj_bias,
            grad_hidden_bias,
            grad_down_bias,
            cond_grads[7],
            cond_grads[8],
            grad_final,
            grad_final_bias,
            grad_align,
            grad_align_bias,
        ]
    )
    flat_grad = jnp.concatenate(
        [gradient_part.reshape(-1) for gradient_part in grad_list]
        + [jnp.zeros((ADAM_PAD - ADAM_LEN,), jnp.float32)]
    )
    grad_model = jnp.concatenate(
        [
            grad_qkv.reshape(D, 3, D).transpose(1, 0, 2),
            grad_proj[None],
            grad_up.reshape(D, fc_ratio, D).transpose(1, 0, 2),
            grad_down.reshape(fc_ratio, D, D),
        ],
        axis=0,
    )
    grad_slot = jnp.take(grad_model, owner_map, axis=0)
    flat_owned = lax.psum_scatter(flat_grad, ("dp", "shard"), scatter_dimension=0, tiled=True)
    loss_total = lax.psum(loss_local, ("dp", "shard"))
    summed = lax.psum(grad_slot, "dp")
    owned = lax.psum_scatter(
        summed.astype(jnp.bfloat16), "shard", scatter_dimension=0, tiled=True
    ).astype(jnp.float32)
    new_left = STAT_BETA * stat_left + (1.0 - STAT_BETA) * jnp.einsum(
        "bij,bkj->bik", owned, owned, precision=HIGHEST
    )
    new_right = STAT_BETA * stat_right + (1.0 - STAT_BETA) * jnp.einsum(
        "bji,bjk->bik", owned, owned, precision=HIGHEST
    )
    left_applied = jnp.einsum("bij,bjk->bik", root_left, owned, precision=HIGHEST)
    direction = jnp.einsum("bij,bjk->bik", left_applied, root_right, precision=HIGHEST)
    root_mean = jnp.sqrt(jnp.mean(direction * direction, axis=(1, 2), keepdims=True))
    block_update = -SHAMPOO_RATE * (direction / (root_mean + RMS_EPS) + DECAY_RATE * blocks_w)
    new_m = BETA_ONE * adam_m + (1.0 - BETA_ONE) * flat_owned
    new_v = BETA_TWO * adam_v + (1.0 - BETA_TWO) * flat_owned * flat_owned
    corrected_m = new_m / (1.0 - BETA_ONE**STEP)
    corrected_v = new_v / (1.0 - BETA_TWO**STEP)
    adam_update = -ADAM_RATE * (
        corrected_m / (jnp.sqrt(corrected_v) + ADAM_EPS) + DECAY_RATE * adam_flat
    )
    return (loss_total, block_update, new_left, new_right, adam_update, new_m, new_v)


def solution(mesh):
    return jax.shard_map(
        body,
        mesh=mesh,
        in_specs=(
            P(("dp", "shard"), None, None),
            P(("dp", "shard"), None, None),
            P(("dp", "shard")),
            P(("dp", "shard")),
            P(("dp", "shard")),
            P(("dp", "shard"), None, None),
            P(),
            P(("dp", "shard")),
            P(("dp", "shard")),
            P(("dp", "shard")),
            P("shard", None, None),
            P("shard", None, None),
            P("shard", None, None),
            P("shard", None, None),
            P("shard", None, None),
        ),
        out_specs=(
            P(),
            P("shard", None, None),
            P("shard", None, None),
            P("shard", None, None),
            P(("dp", "shard")),
            P(("dp", "shard")),
            P(("dp", "shard")),
        ),
        check_vma=False,
    )
```

profile of v0, /device:TPU:0, one launch (start us, length us, event | category | flops | bytes accessed | tf_op | source)
XLA Modules:
  0.0 795.7 jit_solution(3456417252762726016)
XLA Ops:
  17.3 26.3 %all-gather.5.cloned.1.call-done = bf16[12,384,384]{2,1,0:T(8,128)(2,1)} async-done(((bf16[3,384,384]{2,1,0:T(8,128)(2,1)}), bf16[12,384,384]{2,1,0:T(8,128)(2,1)}) %all-gather.5.cloned.1.call-update) | async-done | bytes 3538960 | tf_op jit(solution)/shard_map/all_gather | solution.py:175
  43.6 5.1 gather_fusion
  54.7 54.4 %all-gather.3.cloned.1.call-done = bf16[2129920]{0:T(1024)(128)(2,1)} async-done(((bf16[66560]{0:T(1024)(128)(2,1)}), bf16[2129920]{0:T(1024)(128)(2,1)}) %all-gather.3.cloned.1.call-update) | async-done | bytes 4259856 | tf_op jit(solution)/shard_map/all_gather | solution.py:174
  122.9 3.5 reshape.435
  140.8 4.3 copy.90
  145.1 5.7 reshape.436
  159.2 3.6 fusion.106
  169.7 3.8 fusion.104
  187.9 7.3 fusion.13
  195.2 5.1 convert_reduce_fusion
  200.4 3.1 fusion.33
  203.6 3.5 multiply_reduce_fusion.2
  210.1 3.0 convert_reduce_fusion.4
  218.7 3.0 reshape.446
  221.8 7.7 multiply_reduce_fusion
  229.5 6.3 multiply_convert_fusion
  252.3 4.8 fusion.95
  265.3 3.4 fusion.46
  271.5 3.4 copy.104
  276.3 4.7 reshape.451
  300.4 87.2 %concatenate.35 = f32[2129920]{0:T(1024)} concatenate(f32[6144]{0:T(1024)} %reshape.447, f32[384]{0:T(512)} %get-tuple-element.39, f32[98304]{0:T(1024)S(1)} %copy-done.57, f32[384]{0:T(512)} %get-tuple-element.37, f32[147456]{0:T(1024)S(1)} %reshape.449, f32[384]{0:T(512)} %get-tuple-element.110, f32[384384]{0:T(1024)} %reshape.450, f32[884736]{0:T(1024)} %reshape.451, ...), dimensions={0} | concatenate | bytes 17039360 | tf_op jit(solution)/shard_map/concatenate | solution.py:384
  391.2 4.9 copy.131
  396.1 5.1 convolution_bitcast_fusion
  401.2 4.7 copy.132
  406.0 4.2 fusion.114
  410.2 3.3 pad_maximum_fusion
  413.4 7.0 gather_fusion.1
  420.5 6.6 broadcast_select_fusion
  427.0 306.1 %all-reduce.5 = bf16[12,384,384]{2,1,0:T(8,128)(2,1)} all-reduce(f32[12,384,384]{2,1,0:T(8,128)} %broadcast_select_fusion), channel_id=1, replica_groups=mesh['dp'=8,'shard'=4] {'dp'}, use_global_device_ids=true, to_apply=%region_20.21 | all-reduce | flops 1769472 | bytes 10616832 | tf_op jit(solution)/shard_map/psum | solution.py:400
  734.6 38.9 %psum.14 = f32[]{:T(128)} all-reduce(f32[]{:T(128)S(6)} %sub.143), channel_id=1, replica_groups=mesh['dp'=8,'shard'=4] {'dp','shard'}, use_global_device_ids=true, to_apply=%region_14.15 | all-reduce | flops 1 | bytes 8 | tf_op jit(solution)/shard_map/psum | solution.py:399
  775.6 3.0 fusion.115
  778.7 3.8 multiply_reduce_fusion.3
  (360 shorter events, 142.3 us)
Async XLA Ops:
  7.2 771.5 %copy-start = (f32[3,384,384]{2,1,0:T(8,128)S(1)}, f32[3,384,384]{2,1,0:T(8,128)}, u32[]{:S(2)}) copy-start(f32[3,384,384]{2,1,0:T(8,128)} %param.29) | copy-start | bytes 5308420
  7.2 5.1 copy-start.22
  7.2 36.4 %all-gather.5.cloned.1.call-start = ((), (), s32[]{:S(2)}) async-start(), calls=%async_computation.2 | async-start | bytes 4423680 | tf_op jit(solution)/shard_map/all_gather | solution.py:175
  9.9 99.2 %all-gather.3.cloned.1.call-start = ((), (), s32[]{:S(2)}) async-start(), calls=%async_computation.1 | async-start | bytes 4392960 | tf_op jit(solution)/shard_map/all_gather | solution.py:174
  11.6 5.1 copy-start.98
  11.6 5.1 copy-start.96
  11.6 761.8 %all-reduce.4.cloned.1.call-start = ((), (), s32[]{:S(2)}) async-start(), calls=%async_computation.4 | async-start | bytes 17039360
  17.3 114.6 %copy-start.88 = (f32[4,128]{1,0:T(4,128)}, f32[4,128]{1,0:T(4,128)S(1)}, u32[]{:S(2)}) copy-start(f32[4,128]{1,0:T(4,128)S(1)} %get-tuple-element.90) | copy-start | bytes 6148
  17.3 114.6 %copy-start.90 = (f32[4,128]{1,0:T(4,128)}, f32[4,128]{1,0:T(4,128)S(1)}, u32[]{:S(2)}) copy-start(f32[4,128]{1,0:T(4,128)S(1)} %get-tuple-element.91) | copy-start | bytes 6148
  169.7 6.8 copy-start.82
  177.9 4.8 copy-start.91
  180.7 7.1 slice-start.2
  182.7 5.2 slice-start.3
  187.8 7.4 copy-start.66
  195.2 5.1 copy-start.3
  195.2 5.1 copy-start.59
  195.2 5.1 copy-start.61
  195.2 5.1 copy-start.63
  195.2 5.1 copy-start.65
  221.8 17.5 %slice-start = ((s8[6291456]{0:T(1024)(128)(4,1)}), s8[4194304]{0:T(1024)(128)(4,1)S(1)}, s32[]{:S(2)}) async-start(s8[6291456]{0:T(1024)(128)(4,1)} %bitcast.283), calls=%async_computation.5 | async-start | bytes 8388608
  229.5 6.4 copy-start.26
  229.5 9.8 %slice-start.1 = ((s8[6291456]{0:T(1024)(128)(4,1)}), s8[2097152]{0:T(1024)(128)(4,1)S(1)}, s32[]{:S(2)}) async-start(s8[6291456]{0:T(1024)(128)(4,1)} %bitcast.283), calls=%async_computation.6 | async-start | bytes 4194304
  252.2 5.3 copy-start.18
  257.6 6.1 copy-start.50
  257.6 7.7 copy-start.4
  265.3 6.2 copy-start.16
  282.3 8.4 %copy-start.38 = (f32[384,768]{1,0:T(8,128)S(1)}, f32[384,768]{1,0:T(8,128)}, u32[]{:S(2)}) copy-start(f32[384,768]{1,0:T(8,128)} %fusion.46) | copy-start | bytes 3538948
  291.8 6.4 copy-start.33
  291.8 8.6 %copy-start.57 = (f32[98304]{0:T(1024)S(1)}, f32[98304]{0:T(1024)}, u32[]{:S(2)}) copy-start(f32[98304]{0:T(1024)} %reshape.448) | copy-start | bytes 1179652
  387.6 388.0 %reduce-scatter.2.cloned.1.call-start = ((), (), s32[]{:S(2)}) async-start(), calls=%async_computation.3 | async-start | bytes 4423680 | tf_op jit(solution)/shard_map/reduce_scatter | solution.py:401
  413.4 7.0 copy-start.95
  733.1 42.5 %copy-start.54 = (f32[3,384,384]{2,1,0:T(8,128)S(1)}, f32[3,384,384]{2,1,0:T(8,128)}, u32[]{:S(2)}) copy-start(f32[3,384,384]{2,1,0:T(8,128)} %param.28) | copy-start | bytes 5308420
  (75 other events, 205.7 us)
Sparse Core Ops, SparseCore 0:
  10.1 33.4 all-gather.4
  47.1 61.9 all-gather.2
  387.7 243.6 all-reduce.3
  733.2 39.6 reduce-scatter.1
where the time goes:
time: 809 us; the launch traced here: 796 us
  blocking collectives  345 us (43%)
  local copies, waits for them, and re-layouts  186 us (23%)
  matrix products  103 us (13%)
  waiting for transfers between devices  80.8 us (10%)
  other arithmetic  64.7 us (8%)
  between operations  16.6 us (2%)
    psum x1, blocking collectives, body(): summed = lax.psum(grad_slot, 'dp')  306 us
    concatenate x1, local copies, waits for them, and re-layouts, body(): jnp.concatenate([gradient_part.reshape(-1) for gradient_part in grad_list...  87.2 us
    dot_general x20, matrix products, matmul(): return jnp.dot(left, right, preferred_element_type=jnp.float32)  57.1 us
    all_gather x1, waiting for transfers between devices, body(): lax.all_gather(adam_flat.astype(jnp.bfloat16), ('dp', 'shard'), axis=0, t...  54.4 us
    psum x1, blocking collectives, body(): loss_total = lax.psum(loss_local, ('dp', 'shard'))  38.9 us
    all_gather x1, waiting for transfers between devices, body(): lax.all_gather(blocks_w.astype(jnp.bfloat16), 'shard', axis=0, tiled=True)  26.3 us
  transfers between devices with their start and end apart: 4, of which 2 were waited for; matrix products, arithmetic and copies ran while one was open for 7% of the time, Pallas kernels for 0%

commit v1 on v0

v1 whole, which is shorter than its diff:
```python
import functools
import math

import jax
import jax.numpy as jnp
from jax import lax
from jax.experimental import pallas as pl
from jax.experimental.pallas import tpu as pltpu
from jax.sharding import PartitionSpec as P

D = 384
HEADS = 6
HDIM = 64
F = 1536
PD = 16
GRID = 16
SEQ = 256
FREQ = 256
NCLS = 1001
DINO = 768
STEP = 10
NBLK = 12
ADAM_LEN = 2125072
ADAM_PAD = 2129920

BETA_ONE = 0.9
BETA_TWO = 0.95
ADAM_EPS = 1e-08
ADAM_RATE = 0.01
DECAY_RATE = 0.1
STAT_BETA = 0.9
SHAMPOO_RATE = 0.02
RMS_EPS = 1e-08
REPA_WEIGHT = 0.5
NORM_EPS = 1e-06
QK_SCALE = HDIM ** (-0.5)

AXES = ("dp", "shard")
BF = jnp.bfloat16
F32 = jnp.float32
VM = pl.BlockSpec(memory_space=pltpu.VMEM)
SM = pl.BlockSpec(memory_space=pltpu.SMEM)

FLAT_ROWS = ADAM_PAD // 128
R_PATCH = 0
R_PATCH_B = 48
R_TIME_IN = 51
R_TIME_IN_B = 819
R_TIME_OUT = 822
R_TIME_OUT_B = 1974
R_CLASS = 1977
R_MOD = 4980
R_MOD_B = 11892
R_QUERY_B = 11910
R_VALUE_B = 11913
R_PROJ_B = 11916
R_HIDDEN_B = 11919
R_DOWN_B = 11931
R_FMOD = 11934
R_FMOD_B = 14238
R_FINAL = 14244
R_FINAL_B = 14292
ALIGN_ROWS = 2310

MISC = 256
PAY = 56


def shape(dims, kind=F32):
    return jax.ShapeDtypeStruct(dims, kind)


def mm(left, right):
    return jnp.dot(left, right, preferred_element_type=F32)


def mm_nt(left, right):
    return lax.dot_general(left, right, (((1,), (1,)), ((), ())), preferred_element_type=F32)


def mm_tn(left, right):
    return lax.dot_general(left, right, (((0,), (0,)), ((), ())), preferred_element_type=F32)


def silu(v):
    return v / (1.0 + jnp.exp(-v))


def silu_slope(v):
    s = 1.0 / (1.0 + jnp.exp(-v))
    return s * (1.0 + v * (1.0 - s))


def split3(v):
    one = v.astype(BF)
    rest = v - one.astype(F32)
    two = rest.astype(BF)
    return one, two, (rest - two.astype(F32)).astype(BF)


def stack3(v):
    one, two, three = split3(v)
    return jnp.concatenate([one.astype(F32), two.astype(F32), three.astype(F32)], axis=0).astype(BF)


def fold3(v):
    third = v.shape[0] // 3
    return v[:third] + v[third : 2 * third] + v[2 * third :]


def place_of(z, x, y, c):
    return ((z * 2 + x) * 2 + y) * 2 + c


def permutation(move):
    pairs = []
    for z in range(4):
        for x in range(2):
            for y in range(2):
                for c in range(2):
                    pairs.append((place_of(z, x, y, c), place_of(*move(z, x, y, c))))
    return pairs


TO_C = permutation(lambda z, x, y, c: (z, x, y, 1 - c))
TO_Y = permutation(lambda z, x, y, c: (z, x, 1 - y, c))
TO_X = permutation(lambda z, x, y, c: (z, 1 - x, y, c))
TO_Z = [permutation(lambda z, x, y, c, d=d: ((z + d) % 4, x, y, c)) for d in range(4)]


def send(value, pairs):
    return lax.ppermute(value, AXES, pairs)


def coordinates():
    dp = lax.axis_index("dp")
    sh = lax.axis_index("shard")
    return dp // 2, dp % 2, sh // 2, sh % 2


def pick(array, start, size):
    return lax.dynamic_slice_in_dim(array, start, size, 0)


def gather_all(piece, cut):
    turned = [piece] + [send(piece, TO_Z[d]) for d in (1, 2, 3)]
    first = jnp.stack([t[:cut] for t in turned])
    second = jnp.stack([t[cut:] for t in turned])
    first_x = send(first, TO_X)
    second_y = send(second, TO_Y)
    first = jnp.concatenate([first, first_x])
    second = jnp.concatenate([second, second_y])
    parts = [first, second, send(first, TO_Y), send(second, TO_X)]
    return parts + [send(p, TO_C) for p in parts]


def flip(value, bit):
    return 1 - value if bit else value


def gather_places(cut):
    def maker(dc, kind):
        def entry(i, at):
            z, x, y, c = at
            dz, far = i % 4, i // 4
            dx, dy = {0: (far, 0), 1: (0, far), 2: (far, 1), 3: (1, far)}[kind]
            return place_of(lax.rem(z + 4 - dz, 4), flip(x, dx), flip(y, dy), flip(c, dc))
        return entry

    offsets = [0, cut, 0, cut]
    return [(offsets[k], maker(dc, k)) for dc in (0, 1) for k in range(4)]


def read_coordinates(ref):
    return ref[0], ref[1], ref[2], ref[3]


def cond_kernel(places, rows, at_ref, cls_ref, feat_ref, *refs):
    count = len(places)
    pieces = refs[:count]
    (mods_ref, pre_ref, th_ref, cond_ref, modw_ref, fmodw_ref, tout_ref, align_ref, bias_ref,
     patch_ref, final_ref, flat, rolled) = refs[count:]
    at = read_coordinates(at_ref)
    for ref, (offset, entry) in zip(pieces, places):
        for i in range(ref.shape[0]):
            start = pl.multiple_of(entry(i, at) * rows + offset, 8)
            flat[pl.ds(start, ref.shape[1]), :] = ref[i].astype(F32)

    def row(first, count):
        return jnp.concatenate([flat[first + l : first + l + 1, :] for l in range(count)], axis=1)

    def columns(first, depth, count, which):
        return flat[pl.ds(first + which, depth, stride=count), :].astype(BF)

    def wide(v, first, depth, count, keep=None):
        stacked = stack3(v)
        out = []
        for j in range(count):
            w = columns(first, depth, count, j)
            if keep is not None:
                keep[:, 128 * j : 128 * j + 128] = w
            out.append(fold3(mm(stacked, w)))
        return jnp.concatenate(out, axis=1)

    pre = wide(feat_ref[...], R_TIME_IN, FREQ, 3) + row(R_TIME_IN_B, 3)
    th = silu(pre)
    picked = []
    for m in range(4):
        r = R_CLASS + 3 * cls_ref[m]
        picked.append(jnp.concatenate([flat[pl.ds(r + l, 1), :] for l in range(3)], axis=1))
    picked = jnp.concatenate(picked + [jnp.zeros((4, D), F32)], axis=0)
    cond = wide(th, R_TIME_OUT, D, 3, tout_ref) + row(R_TIME_OUT_B, 3) + picked
    act = silu(cond)
    pre_ref[...] = pre
    th_ref[...] = th
    cond_ref[...] = cond
    mods_ref[:, : 6 * D] = wide(act, R_MOD, D, 18, modw_ref) + row(R_MOD_B, 18)
    mods_ref[:, 6 * D :] = wide(act, R_FMOD, D, 6, fmodw_ref) + row(R_FMOD_B, 6)

    spot = lax.broadcasted_iota(jnp.int32, (ALIGN_ROWS, 128), 1)
    here = pltpu.roll(flat[R_FINAL_B : R_FINAL_B + ALIGN_ROWS, :], 112, 1)
    after = pltpu.roll(flat[R_FINAL_B + 1 : R_FINAL_B + 1 + ALIGN_ROWS, :], 112, 1)
    rolled[...] = jnp.where(spot < 112, here, after)
    for j in range(6):
        align_ref[:, 128 * j : 128 * j + 128] = rolled[pl.ds(j, D, stride=6), :].astype(BF)

    bias_ref[...] = jnp.zeros_like(bias_ref)
    for at_row, first in ((0, R_PATCH_B), (1, R_QUERY_B), (2, R_VALUE_B), (3, R_PROJ_B),
                          (4, R_HIDDEN_B), (5, R_HIDDEN_B + 3), (6, R_HIDDEN_B + 6),
                          (7, R_HIDDEN_B + 9), (8, R_DOWN_B)):
        bias_ref[at_row : at_row + 1, :] = row(first, 3)
    for half in range(2):
        bias_ref[9 + half : 10 + half, :] = jnp.concatenate(
            [rolled[2304 + 3 * half + l : 2305 + 3 * half + l, :] for l in range(3)], axis=1)
    lane = lax.broadcasted_iota(jnp.int32, (1, 128), 1)
    bias_ref[11:12, :128] = jnp.where(lane < PD, flat[R_FINAL_B : R_FINAL_B + 1, :], 0.0)
    patch = [flat[pl.ds(R_PATCH + l, PD, stride=3), :] for l in range(3)]
    patch_ref[...] = jnp.concatenate(patch, axis=1).astype(BF)
    spread = (lax.broadcasted_iota(jnp.int32, (D, 48), 0) // 8
              == lax.broadcasted_iota(jnp.int32, (D, 48), 1)).astype(F32).astype(BF)
    wide_rows = mm(spread, flat[R_FINAL : R_FINAL + 48, :].astype(BF))
    keep = (lax.broadcasted_iota(jnp.int32, (D, 128), 1) // PD
            == lax.broadcasted_iota(jnp.int32, (D, 128), 0) % 8)
    fold = (lax.broadcasted_iota(jnp.int32, (128, 128), 0) % PD
            == lax.broadcasted_iota(jnp.int32, (128, 128), 1)).astype(F32).astype(BF)
    final_ref[...] = mm(jnp.where(keep, wide_rows, 0.0).astype(BF), fold).astype(BF)


def conditioning(at, classes, features, pieces, places, rows):
    kernel = functools.partial(cond_kernel, places, rows)
    return pl.pallas_call(
        kernel,
        name="conditioning",
        out_shape=(shape((8, 8 * D)), shape((8, D)), shape((8, D)), shape((8, D)),
                   shape((D, 6 * D), BF), shape((D, 2 * D), BF), shape((D, D), BF),
                   shape((D, DINO), BF), shape((16, D)), shape((PD, D), BF), shape((D, 128), BF)),
        in_specs=[SM, SM, VM] + [VM] * len(pieces),
        out_specs=[VM] * 11,
        scratch_shapes=[pltpu.VMEM((FLAT_ROWS + 8, 128), F32), pltpu.VMEM((ALIGN_ROWS, 128), F32)],
        cost_estimate=pl.CostEstimate(flops=10**9, bytes_accessed=10**7, transcendentals=0),
    )(at, classes, features, *pieces)


def blocks_kernel(at_ref, own_ref, mine_ref, pair_ref, near_ref, far_ref, near_c_ref, far_c_ref, out_ref):
    z, x, y, c = read_coordinates(at_ref)
    for t in range(3):
        out_ref[own_ref[3 * (2 * y + c) + t]] = mine_ref[t]
        out_ref[own_ref[3 * (2 * y + 1 - c) + t]] = pair_ref[t]
        over = own_ref[3 * (2 * (1 - y) + c) + t]
        over_c = own_ref[3 * (2 * (1 - y) + 1 - c) + t]
        for side in range(2):
            @pl.when(x == side)
            def _():
                low, high = 192 * side, 192 * (1 - side)
                out_ref[over, low : low + 192, :] = near_ref[t]
                out_ref[over, high : high + 192, :] = far_ref[t]
                out_ref[over_c, low : low + 192, :] = near_c_ref[t]
                out_ref[over_c, high : high + 192, :] = far_c_ref[t]


def gather_blocks(at, owner_map, mine):
    x = lax.rem(lax.axis_index("dp"), 2)
    half = lax.dynamic_slice_in_dim(mine, 192 * x, 192, 1)
    near = send(half, TO_Y)
    far = send(near, TO_X)
    pair = send(mine, TO_C)
    near_c = send(near, TO_C)
    far_c = send(far, TO_C)
    return pl.pallas_call(
        blocks_kernel,
        name="gather_blocks",
        out_shape=shape((NBLK, D, D), BF),
        in_specs=[SM, SM] + [VM] * 6,
        out_specs=VM,
        cost_estimate=pl.CostEstimate(flops=0, bytes_accessed=7 * 10**6, transcendentals=0),
    )(at, owner_map, mine, pair, near, far, near_c, far_c)


UNIT = 24
CHIP_ROWS = 7 * UNIT + 8


def unit_of(z, x, y):
    return jnp.where(z < 2, x * 4 + y * 2 + z, 6 + y * 4 + x * 2 + z)


def add_low(left, right):
    return (left.astype(F32) + right.astype(F32)).astype(BF)


def reduce_units(units):
    z, x, y, c = coordinates()
    got = send(pick(units, 1 - c, 1)[0], TO_C)
    both = add_low(pick(units, c, 1)[0], got)
    first, second = both[:8], both[8:]
    got_x = send(pick(first, 4 * (1 - x), 4), TO_X)
    got_y = send(pick(second, 4 * (1 - y), 4), TO_Y)
    first = add_low(pick(first, 4 * x, 4), got_x)
    second = add_low(pick(second, 4 * y, 4), got_y)
    got_y = send(pick(first, 2 * (1 - y), 2), TO_Y)
    got_x = send(pick(second, 2 * (1 - x), 2), TO_X)
    quarter = jnp.concatenate(
        [add_low(pick(first, 2 * y, 2), got_y), add_low(pick(second, 2 * x, 2), got_x)])
    got = [send(pick(quarter, (z + d) % 4, 1)[0], TO_Z[d]) for d in (1, 2, 3)]
    total = pick(quarter, z, 1)[0].astype(F32)
    for g in got:
        total = total + g.astype(F32)
    return total.astype(BF)


def gather_owned(mine, owner_map):
    z, x, y, c = coordinates()
    pair = send(mine, TO_C)
    whole = jnp.where(c == 0, jnp.concatenate([mine, pair]), jnp.concatenate([pair, mine]))
    slots = jnp.take(whole, owner_map, axis=0).reshape(2, 2, 3, UNIT, D)
    slots = lax.dynamic_index_in_dim(slots, c, 1, keepdims=False)
    near = send(lax.dynamic_index_in_dim(slots, 1 - y, 0, keepdims=False), TO_Y)
    both = jnp.stack([lax.dynamic_index_in_dim(slots, y, 0, keepdims=False), near])
    column = jnp.stack([both] + [send(both, TO_Z[d]) for d in (1, 2, 3)])
    return column, send(column, TO_X)


def place_kernel(places, at_ref, *refs):
    pieces = refs[: len(places)]
    pay_ref, align_ref, misc_ref = refs[len(places) :]
    at = read_coordinates(at_ref)
    for ref, (offset, entry) in zip(pieces, places):
        for i in range(ref.shape[0]):
            dev = entry(i, at)
            z, x, y, c = dev // 8, (dev // 4) % 2, (dev // 2) % 2, dev % 2
            unit = unit_of(z, x, y)
            value = ref[i].astype(F32)
            if offset == 0:
                pay_ref[dev, 0:48, :] = value
            else:
                pay_ref[dev, 48:PAY, :] = value[0:8]
                align_ref[c, pl.ds(pl.multiple_of(unit * UNIT, 8), UNIT), :] = value[8:32]
                misc_ref[pl.ds(pl.multiple_of(c * 128 + unit * 8, 8), 8), :] = value[32:40]


def adam_kernel(local, pay_ref, align_ref, misc_ref, *refs):
    if local:
        at_ref, w_ref, m_ref, v_ref, loss_ref, upd_ref, new_m_ref, new_v_ref, flat, rolled = refs
    else:
        loss_ref, flat, rolled = refs
    rows = 8 * pay_ref.shape[0]

    def tile(j):
        return pay_ref[:, 8 * j : 8 * j + 8, :].reshape(rows, D)

    upper = lax.broadcasted_iota(jnp.int32, (rows, 1), 0) % 8 < 4

    def first(v):
        return jnp.where(upper, v, 0.0)

    def second(v):
        return jnp.where(upper, 0.0, v)

    def put_row(v, row):
        for l in range(v.shape[1] // 128):
            flat[row + l : row + l + 1, :] = v[:, 128 * l : 128 * l + 128]

    def put_matrix(v, row, count, which, height):
        for l in range(v.shape[1] // 128):
            flat[pl.ds(row + which + l, height, stride=count), :] = v[:, 128 * l : 128 * l + 128]

    def total(v):
        return jnp.sum(v, axis=0, keepdims=True)

    last = tile(6)
    ids = second(last[:, 2 * 128 :])
    numbers = (ids[:, 0:1] * 256.0 + ids[:, 1:2]).astype(jnp.int32)
    loss_ref[...] = total(ids[:, 2:3]) + total(ids[:, 3:4]) + total(ids[:, 4:5])

    g_pre = second(tile(5))
    put_matrix(mm_tn(last[:, :FREQ].astype(BF), g_pre.astype(BF)), R_TIME_IN, 3, 0, FREQ)
    put_row(total(g_pre), R_TIME_IN_B)
    g_cond = second(tile(4))
    g_cond_low = g_cond.astype(BF)
    put_matrix(mm_tn(tile(3).astype(BF), g_cond_low), R_TIME_OUT, 3, 0, D)
    put_row(total(g_cond), R_TIME_OUT_B)
    for part in range(3):
        height = 336 if part < 2 else 329
        marks = lax.broadcasted_iota(jnp.int32, (rows, 336), 1) + 336 * part
        hits = second(jnp.where(marks == numbers, 1.0, 0.0)).astype(BF)
        put_matrix(mm_tn(hits, g_cond_low)[:height], R_CLASS + 3 * 336 * part, 3, 0, height)
    act = tile(0)
    act_first = first(act).astype(BF)
    act_second = second(act).astype(BF)
    for t in range(6):
        g = tile(1 + t)
        put_matrix(mm_tn(act_first, g.astype(BF)), R_MOD, 18, 3 * t, D)
        put_row(total(first(g)), R_MOD_B + 3 * t)
    for t in range(2):
        g = tile(1 + t)
        put_matrix(mm_tn(act_second, g.astype(BF)), R_FMOD, 6, 3 * t, D)
        put_row(total(second(g)), R_FMOD_B + 3 * t)

    for l in range(3):
        lanes = slice(128 * l, 128 * l + 128)
        flat[pl.ds(R_PATCH + l, PD, stride=3), :] = misc_ref[0:PD, lanes]
        flat[pl.ds(R_FINAL + l, PD, stride=3), :] = misc_ref[32:48, lanes]
    for at_row, row in ((16, R_PATCH_B), (17, R_QUERY_B), (18, R_VALUE_B), (19, R_PROJ_B),
                        (20, R_HIDDEN_B), (21, R_HIDDEN_B + 3), (22, R_HIDDEN_B + 6),
                        (23, R_HIDDEN_B + 9), (24, R_DOWN_B)):
        put_row(misc_ref[at_row : at_row + 1, :], row)
    rolled[0:8, :] = jnp.zeros((8, 128), F32)
    rolled[8 + ALIGN_ROWS :, :] = jnp.zeros_like(rolled[8 + ALIGN_ROWS :, :])
    rolled[7:8, :] = pltpu.roll(misc_ref[27:28, 0:128], 112, 1)
    for half in range(2):
        for l in range(3):
            rolled[pl.ds(8 + 3 * half + l, D, stride=6), :] = align_ref[half, :, 128 * l : 128 * l + 128]
            r = 8 + 2304 + 3 * half + l
            rolled[r : r + 1, :] = misc_ref[25 + half : 26 + half, 128 * l : 128 * l + 128]
    count = FLAT_ROWS - R_FINAL_B
    spot = lax.broadcasted_iota(jnp.int32, (count, 128), 1)
    here = pltpu.roll(rolled[8 : 8 + count, :], 16, 1)
    before = pltpu.roll(rolled[7 : 7 + count, :], 16, 1)
    flat[R_FINAL_B:FLAT_ROWS, :] = jnp.where(spot < 16, before, here)

    if local:
        z, x, y, c = read_coordinates(at_ref)
        size = w_ref.shape[0]
        start = pl.multiple_of(place_of(z, x, y, c) * size, 8)
        adam_step(flat[pl.ds(start, size), :], w_ref, m_ref, v_ref, upd_ref, new_m_ref, new_v_ref)


def adam_step(grad, w_ref, m_ref, v_ref, upd_ref, new_m_ref, new_v_ref):
    new_m = BETA_ONE * m_ref[...] + (1.0 - BETA_ONE) * grad
    new_v = BETA_TWO * v_ref[...] + (1.0 - BETA_TWO) * grad * grad
    new_m_ref[...] = new_m
    new_v_ref[...] = new_v
    right_m = new_m / (1.0 - BETA_ONE**STEP)
    right_v = new_v / (1.0 - BETA_TWO**STEP)
    upd_ref[...] = -ADAM_RATE * (right_m / (jnp.sqrt(right_v) + ADAM_EPS) + DECAY_RATE * w_ref[...])


ROLL_ROWS = 8 + FLAT_ROWS - R_FINAL_B + 8


def adam_near(at, parts, flat_w, m, v):
    places = gather_places(48)
    pay, align, misc = pl.pallas_call(
        functools.partial(place_kernel, places),
        name="place_gradients",
        out_shape=(shape((32, PAY, D)), shape((2, D, D)), shape((MISC, D))),
        in_specs=[SM] + [VM] * len(parts),
        out_specs=[VM] * 3,
    )(at, *parts)
    size = flat_w.shape
    loss, upd, new_m, new_v = pl.pallas_call(
        functools.partial(adam_kernel, True),
        name="adam",
        out_shape=(shape((1, 1)), shape(size), shape(size), shape(size)),
        in_specs=[VM, VM, VM, SM, VM, VM, VM],
        out_specs=[VM] * 4,
        scratch_shapes=[pltpu.VMEM((FLAT_ROWS, 128), F32), pltpu.VMEM((ROLL_ROWS, 128), F32)],
        cost_estimate=pl.CostEstimate(flops=10**9, bytes_accessed=10**7, transcendentals=0),
    )(pay, align, misc, at, flat_w, m, v)
    return loss[0, 0], upd, new_m, new_v


def adam_wide(pay, align, misc, flat_w, m, v):
    loss, flat = pl.pallas_call(
        functools.partial(adam_kernel, False),
        name="adam_gradient",
        out_shape=(shape((1, 1)), shape((FLAT_ROWS, 128))),
        in_specs=[VM] * 3,
        out_specs=[VM] * 2,
        scratch_shapes=[pltpu.VMEM((ROLL_ROWS, 128), F32)],
    )(pay, align, misc)
    size = flat_w.shape[0]
    place = lax.axis_index("dp") * lax.axis_size("shard") + lax.axis_index("shard")
    grad = lax.dynamic_slice_in_dim(flat, place * size, size, 0)
    upd, new_m, new_v = pl.pallas_call(
        lambda g, *refs: adam_step(g[...], *refs),
        name="adam",
        out_shape=(shape(flat_w.shape),) * 3,
        in_specs=[VM] * 4,
        out_specs=[VM] * 3,
    )(grad, flat_w, m, v)
    return loss[0, 0], upd, new_m, new_v


def shampoo_kernel(near, at_ref, *refs):
    if near:
        column_ref, far_ref, w_ref, sl_ref, sr_ref, rl_ref, rr_ref, upd_ref, nl_ref, nr_ref, grad = refs
        z, x, y, c = read_coordinates(at_ref)
        t = pl.program_id(0)
        for dx in range(2):
            ref = (column_ref, far_ref)[dx]
            for dz in range(4):
                for dy in range(2):
                    unit = unit_of(lax.rem(z + 4 - dz, 4), flip(x, dx), flip(y, dy))
                    rows = pl.ds(pl.multiple_of(unit * UNIT, 8), UNIT)
                    grad[rows, :] = ref[dz, dy, t].astype(F32)
        g = grad[...].astype(BF)
    else:
        grad_ref, w_ref, sl_ref, sr_ref, rl_ref, rr_ref, upd_ref, nl_ref, nr_ref = refs
        g = grad_ref[0]
    nl_ref[0] = STAT_BETA * sl_ref[0] + (1.0 - STAT_BETA) * mm_nt(g, g)
    nr_ref[0] = STAT_BETA * sr_ref[0] + (1.0 - STAT_BETA) * mm_tn(g, g)
    one, two, three = split3(rl_ref[0])
    left = mm(one, g) + (mm(two, g) + mm(three, g))
    l_one, l_two, l_three = split3(left)
    r_one, r_two, r_three = split3(rr_ref[0])
    p = mm(l_one, r_one) + (mm(l_one, r_two) + mm(l_two, r_one)) + (
        mm(l_two, r_two) + mm(l_one, r_three) + mm(l_three, r_one))
    mean = jnp.sum(jnp.sum(p * p, axis=1, keepdims=True), axis=0, keepdims=True) * (1.0 / (D * D))
    root = jnp.sqrt(mean)
    upd_ref[0] = -SHAMPOO_RATE * (p / (root + RMS_EPS) + DECAY_RATE * w_ref[0])


def shampoo(at, grads, blocks_w, stat_left, stat_right, root_left, root_right):
    near = len(grads) == 2
    slots = blocks_w.shape[0]
    one = pl.BlockSpec((1, D, D), lambda t: (t, 0, 0))
    return pl.pallas_call(
        functools.partial(shampoo_kernel, near),
        name="shampoo",
        grid=(slots,),
        out_shape=(shape((slots, D, D)),) * 3,
        in_specs=[SM] + ([VM, VM] if near else [one]) + [one] * 5,
        out_specs=[one] * 3,
        scratch_shapes=[pltpu.VMEM((D, D), F32)] if near else [],
        cost_estimate=pl.CostEstimate(flops=3 * 10**9, bytes_accessed=15 * 10**6, transcendentals=0),
    )(at, *grads, blocks_w, stat_left, stat_right, root_left, root_right)


def position_table():
    quarter = D // 4
    frequencies = 1.0 / 10000.0 ** (jnp.arange(quarter, dtype=jnp.float32) / quarter)
    cell_ids = jnp.arange(SEQ, dtype=jnp.int32)
    row_arg = (cell_ids // GRID).astype(jnp.float32)[:, None] * frequencies[None, :]
    col_arg = (cell_ids % GRID).astype(jnp.float32)[:, None] * frequencies[None, :]
    return jnp.concatenate(
        [jnp.sin(col_arg), jnp.cos(col_arg), jnp.sin(row_arg), jnp.cos(row_arg)], axis=1
    )


def time_features(tstep_idx):
    half_freq = FREQ // 2
    frequencies = jnp.exp(-math.log(10000.0) * jnp.arange(half_freq, dtype=jnp.float32) / half_freq)
    angles = (tstep_idx.astype(jnp.float32) + 0.5)[:, None] * frequencies[None, :]
    return jnp.concatenate([jnp.cos(angles), jnp.sin(angles)], axis=1)


def normalize(values):
    centered = values - jnp.mean(values, axis=-1, keepdims=True)
    inv_dev = lax.rsqrt(jnp.mean(centered * centered, axis=-1, keepdims=True) + NORM_EPS)
    return (centered * inv_dev, inv_dev)


def normalize_back(grad_in, normed, inv_dev):
    return inv_dev * (
        grad_in
        - jnp.mean(grad_in, axis=-1, keepdims=True)
        - normed * jnp.mean(grad_in * normed, axis=-1, keepdims=True)
    )


def cosine_total(aligned, dino_f):
    products = jnp.sum(aligned * dino_f, axis=-1)
    return jnp.sum(
        products
        * lax.rsqrt(jnp.sum(aligned * aligned, axis=-1) + NORM_EPS)
        * lax.rsqrt(jnp.sum(dino_f * dino_f, axis=-1) + NORM_EPS), axis=-1
    )


def row_total(rounded):
    return jnp.sum(rounded.astype(jnp.float32), axis=0)


matmul = mm


def tokens(total_img, noisy, velocity, time_weight, dino, mods, weights, blocks):
    images, seq = noisy.shape[:2]
    rows = images * seq
    bias, patch_low, final_low, align_low = weights
    patch_bias, query_bias, value_bias, proj_bias = bias[0], bias[1], bias[2], bias[3]
    hidden_bias = bias[4:8].reshape(F)
    down_bias = bias[8]
    align_bias = bias[9:11].reshape(DINO)
    final_bias = bias[11, :PD]
    final_low = final_low[:, :PD]
    w_qkv = jnp.concatenate([blocks[0], blocks[1], blocks[2]], axis=1)
    w_proj = blocks[3]
    w_up = jnp.concatenate([blocks[4], blocks[5], blocks[6], blocks[7]], axis=1)
    w_down = blocks[8:].reshape(F, D)
    (shift_one, scale_one, gate_one, shift_two, scale_two, gate_two, final_shift, final_scale) = [
        mods[:, None, which * D : (which + 1) * D] for which in range(8)
    ]
    noisy_low = noisy.astype(jnp.bfloat16).reshape(rows, PD)
    hidden0 = (matmul(noisy_low, patch_low) + patch_bias).reshape(images, seq, D) + position_table()
    norm_one, inv_one = normalize(hidden0)
    act_one = (norm_one * (1.0 + scale_one) + shift_one).astype(jnp.bfloat16).reshape(rows, D)
    qkv_bias = jnp.concatenate([query_bias, jnp.zeros((D,), jnp.float32), value_bias])
    projected = (
        (matmul(act_one, w_qkv) + qkv_bias)
        .astype(jnp.bfloat16)
        .reshape(images, seq, 3, HEADS, HDIM)
    )
    queries = projected[:, :, 0]
    key_part = projected[:, :, 1]
    values = projected[:, :, 2]
    scale_qk = HDIM ** (-0.5)
    scores = (
        jnp.einsum("gqhe,gkhe->ghqk", queries, key_part, preferred_element_type=jnp.float32)
        * scale_qk
    )
    row_max = jnp.max(scores, axis=-1, keepdims=True)
    log_total = row_max + jnp.log(jnp.sum(jnp.exp(scores - row_max), axis=-1, keepdims=True))
    probs_low = jnp.exp(scores - log_total).astype(jnp.bfloat16)
    attended = (
        jnp.einsum("ghqk,gkhe->gqhe", probs_low, values, preferred_element_type=jnp.float32)
        .reshape(rows, D)
        .astype(jnp.bfloat16)
    )
    branch_one = (matmul(attended, w_proj) + proj_bias).reshape(images, seq, D)
    hidden1 = hidden0 + gate_one * branch_one
    norm_two, inv_two = normalize(hidden1)
    act_two = (norm_two * (1.0 + scale_two) + shift_two).astype(jnp.bfloat16).reshape(rows, D)
    inner_pre = matmul(act_two, w_up) + hidden_bias
    gelu_out, gelu_back = jax.vjp(functools.partial(jax.nn.gelu, approximate=True), inner_pre)
    gelu_low = gelu_out.astype(jnp.bfloat16)
    branch_two = (matmul(gelu_low, w_down) + down_bias).reshape(images, seq, D)
    hidden2 = hidden1 + gate_two * branch_two
    norm_three, inv_three = normalize(hidden2)
    act_three = (
        (norm_three * (1.0 + final_scale) + final_shift).astype(jnp.bfloat16).reshape(rows, D)
    )
    output = (matmul(act_three, final_low) + final_bias).reshape(images, seq, PD)
    errors = output - velocity
    main_term = jnp.sum(time_weight[:, None, None] * errors * errors, axis=(1, 2)) / (total_img * SEQ * PD)
    hidden1_low = hidden1.astype(jnp.bfloat16).reshape(rows, D)
    aligned = (matmul(hidden1_low, align_low) + align_bias).reshape(images, seq, DINO)
    dino_f = dino.astype(jnp.float32)
    cosine_sum, cosine_back = jax.vjp(functools.partial(cosine_total, dino_f=dino_f), aligned)
    align_scale = REPA_WEIGHT / (total_img * SEQ)
    loss_local = main_term - align_scale * cosine_sum
    back_output = (
        (2.0 * time_weight[:, None, None] * errors / (total_img * SEQ * PD))
        .reshape(rows, PD)
        .astype(jnp.bfloat16)
    )
    grad_final = matmul(act_three.T, back_output)
    grad_final_bias = row_total(back_output)
    back_three = matmul(back_output, final_low.T).reshape(images, seq, D)
    grad_final_shift = jnp.sum(back_three, axis=1)
    grad_final_scale = jnp.sum(back_three * norm_three, axis=1)
    back_hidden2 = normalize_back(back_three * (1.0 + final_scale), norm_three, inv_three)
    back_branch_two = (back_hidden2 * gate_two).reshape(rows, D).astype(jnp.bfloat16)
    grad_gate_two = jnp.sum(back_hidden2 * branch_two, axis=1)
    grad_down = matmul(gelu_low.T, back_branch_two)
    grad_down_bias = row_total(back_branch_two)
    back_inner = gelu_back(matmul(back_branch_two, w_down.T))[0].astype(jnp.bfloat16)
    grad_up = matmul(act_two.T, back_inner)
    grad_hidden_bias = row_total(back_inner)
    back_two = matmul(back_inner, w_up.T).reshape(images, seq, D)
    grad_shift_two = jnp.sum(back_two, axis=1)
    grad_scale_two = jnp.sum(back_two * norm_two, axis=1)
    back_aligned = cosine_back(jnp.full((images,), -align_scale, jnp.float32))[0].astype(jnp.bfloat16).reshape(rows, DINO)
    grad_align = matmul(hidden1_low.T, back_aligned)
    grad_align_bias = row_total(back_aligned)
    back_hidden1 = (
        back_hidden2
        + normalize_back(back_two * (1.0 + scale_two), norm_two, inv_two)
        + matmul(back_aligned, align_low.T).reshape(images, seq, D)
    )
    back_branch_one = (back_hidden1 * gate_one).reshape(rows, D).astype(jnp.bfloat16)
    grad_gate_one = jnp.sum(back_hidden1 * branch_one, axis=1)
    grad_proj = matmul(attended.T, back_branch_one)
    grad_proj_bias = row_total(back_branch_one)
    back_attended = (
        matmul(back_branch_one, w_proj.T).astype(jnp.bfloat16).reshape(images, seq, HEADS, HDIM)
    )
    back_probs = jnp.einsum(
        "gqhe,gkhe->ghqk", back_attended, values, preferred_element_type=jnp.float32
    )
    grad_values = jnp.einsum(
        "ghqk,gqhe->gkhe", probs_low, back_attended, preferred_element_type=jnp.float32
    )
    scores_again = (
        jnp.einsum("gqhe,gkhe->ghqk", queries, key_part, preferred_element_type=jnp.float32)
        * scale_qk
    )
    probs_again = jnp.exp(scores_again - log_total)
    back_scores = (
        probs_again * (back_probs - jnp.sum(back_probs * probs_again, axis=-1, keepdims=True))
    ).astype(jnp.bfloat16)
    grad_queries = (
        jnp.einsum("ghqk,gkhe->gqhe", back_scores, key_part, preferred_element_type=jnp.float32)
        * scale_qk
    )
    grad_keys = (
        jnp.einsum("ghqk,gqhe->gkhe", back_scores, queries, preferred_element_type=jnp.float32)
        * scale_qk
    )
    back_projected = (
        jnp.stack([grad_queries, grad_keys, grad_values], axis=2)
        .reshape(rows, 3 * D)
        .astype(jnp.bfloat16)
    )
    grad_qkv = matmul(act_one.T, back_projected)
    grad_qkv_bias = row_total(back_projected)
    back_one = matmul(back_projected, w_qkv.T).reshape(images, seq, D)
    grad_shift_one = jnp.sum(back_one, axis=1)
    grad_scale_one = jnp.sum(back_one * norm_one, axis=1)
    back_hidden0 = (
        (back_hidden1 + normalize_back(back_one * (1.0 + scale_one), norm_one, inv_one))
        .reshape(rows, D)
        .astype(jnp.bfloat16)
    )
    grad_patch = matmul(noisy_low.T, back_hidden0)
    grad_patch_bias = row_total(back_hidden0)
    grad_mods = jnp.concatenate(
        [
            grad_shift_one,
            grad_scale_one,
            grad_gate_one,
            grad_shift_two,
            grad_scale_two,
            grad_gate_two,
            grad_final_shift,
            grad_final_scale,
        ],
        axis=1,
    )
    fc_ratio = F // D
    grad_model = jnp.concatenate(
        [
            grad_qkv.reshape(D, 3, D).transpose(1, 0, 2),
            grad_proj[None],
            grad_up.reshape(D, fc_ratio, D).transpose(1, 0, 2),
            grad_down.reshape(fc_ratio, D, D),
        ],
        axis=0,
    ).astype(BF)
    grad_align = grad_align.reshape(D, 2, D).transpose(1, 0, 2).astype(BF)
    zero = jnp.zeros((D,), F32)
    misc = jnp.concatenate([
        grad_patch,
        jnp.stack([grad_patch_bias, grad_qkv_bias[:D], grad_qkv_bias[2 * D :], grad_proj_bias]),
        grad_hidden_bias.reshape(4, D),
        grad_down_bias[None],
        grad_align_bias.reshape(2, D),
        jnp.pad(grad_final_bias, (0, D - PD))[None],
        jnp.zeros((4, D), F32),
        grad_final.reshape(PD, D),
        jnp.zeros((MISC - 48, D), F32),
    ]).astype(BF)
    return loss_local, grad_model, grad_align, misc, grad_mods


def payload(cond_act, th, features, grad_mods, g_cond, g_pre, class_ids, losses):
    images = cond_act.shape[0]
    one, two, three = split3(losses)
    ids = jnp.stack([(class_ids // 256).astype(F32), (class_ids % 256).astype(F32),
                     one.astype(F32), two.astype(F32), three.astype(F32)], axis=1)
    ids = jnp.pad(ids, ((0, 0), (0, 123)))
    first = jnp.concatenate([cond_act, grad_mods[:, : 6 * D]], axis=1)
    second = jnp.concatenate(
        [cond_act, grad_mods[:, 6 * D :], th, g_cond, g_pre, features, ids], axis=1)
    both = jnp.concatenate([first, second], axis=0)
    return both.reshape(2 * images, 7, D).transpose(1, 0, 2).reshape(PAY, D).astype(BF)


def body(
    noisy,
    velocity,
    tstep_idx,
    class_ids,
    time_weight,
    dino,
    owner_map,
    adam_flat,
    adam_m,
    adam_v,
    blocks_w,
    stat_left,
    stat_right,
    root_left,
    root_right,
):
    dp, group = lax.axis_size("dp"), lax.axis_size("shard")
    near = (dp, group) == (8, 4)
    images = noisy.shape[0]
    total_img = images * dp * group
    at = jnp.stack([jnp.asarray(v, jnp.int32) for v in coordinates()])
    flat_w = adam_flat.reshape(-1, 128)
    flat_m = adam_m.reshape(-1, 128)
    flat_v = adam_v.reshape(-1, 128)
    mine = flat_w.astype(BF)
    features = time_features(tstep_idx)
    rows = flat_w.shape[0]
    if near:
        cut = rows // 16 * 8 + 8 if rows // 8 % 2 else rows // 2
        pieces = gather_all(mine, cut)
        places = gather_places(cut)
        blocks = gather_blocks(at, owner_map, blocks_w.astype(BF))
    else:
        pieces = [lax.all_gather(mine, AXES, axis=0, tiled=True)[None]]
        places = [(0, lambda i, at: 0)]
        slot_low = lax.all_gather(blocks_w.astype(BF), "shard", axis=0, tiled=True)
        block_ids = jnp.arange(NBLK, dtype=jnp.int32)
        slot_of = jnp.sum(
            block_ids[:, None] * (owner_map[:, None] == block_ids[None, :]).astype(jnp.int32), axis=0
        )
        blocks = jnp.take(slot_low, slot_of, axis=0)
    (mods, pre, th, cond, mod_w, fmod_w, tout_w, align_low, bias, patch_low, final_low) = conditioning(
        at, class_ids, jnp.pad(features, ((0, 4), (0, 0))), pieces, places, rows)
    mods, pre, th, cond = mods[:images], pre[:images], th[:images], cond[:images]
    losses, grad_model, grad_align, misc, grad_mods = tokens(
        total_img, noisy, velocity, time_weight, dino, mods,
        (bias, patch_low, final_low, align_low), blocks)
    high = lax.Precision.HIGHEST
    g_act = jnp.dot(grad_mods[:, : 6 * D], mod_w.T.astype(F32), precision=high) + jnp.dot(
        grad_mods[:, 6 * D :], fmod_w.T.astype(F32), precision=high)
    g_cond = g_act * silu_slope(cond)
    g_pre = jnp.dot(g_cond, tout_w.T.astype(F32), precision=high) * silu_slope(pre)
    pay = payload(silu(cond), th, features, grad_mods, g_cond, g_pre, class_ids, losses)
    if near:
        units = jnp.concatenate([
            jnp.concatenate([grad_model.reshape(2, 6, D, D), grad_align[:, None]], axis=1)
            .reshape(2, 7, 16, UNIT, D).transpose(0, 2, 1, 3, 4).reshape(2, 16, 7 * UNIT, D),
            misc.reshape(2, 16, 8, D)], axis=2)
        owned = reduce_units(units)
        grads = gather_owned(owned[: 6 * UNIT].reshape(6, UNIT, D), owner_map)
        parts = gather_all(jnp.concatenate([pay, owned[6 * UNIT :]]), 48)
        loss, upd, new_m, new_v = adam_near(at, parts, flat_w, flat_m, flat_v)
    else:
        pays = lax.all_gather(pay, AXES, axis=0, tiled=True).reshape(dp * group, PAY, D).astype(F32)
        align_sum = lax.psum(grad_align.astype(F32), AXES)
        misc_sum = lax.psum(misc.astype(F32), AXES)
        loss, upd, new_m, new_v = adam_wide(pays, align_sum, misc_sum, flat_w, flat_m, flat_v)
        slots = jnp.take(grad_model, owner_map, axis=0)
        owned = lax.psum_scatter(slots, "shard", scatter_dimension=0, tiled=True)
        grads = [lax.psum(owned.astype(F32), "dp").astype(BF)]
    block_update, new_left, new_right = shampoo(
        at, grads, blocks_w, stat_left, stat_right, root_left, root_right)
    return (loss, block_update, new_left, new_right,
            upd.reshape(-1), new_m.reshape(-1), new_v.reshape(-1))


def solution(mesh):
    return jax.shard_map(
        body,
        mesh=mesh,
        in_specs=(
            P(("dp", "shard"), None, None),
            P(("dp", "shard"), None, None),
            P(("dp", "shard")),
            P(("dp", "shard")),
            P(("dp", "shard")),
            P(("dp", "shard"), None, None),
            P(),
            P(("dp", "shard")),
            P(("dp", "shard")),
            P(("dp", "shard")),
            P("shard", None, None),
            P("shard", None, None),
            P("shard", None, None),
            P("shard", None, None),
            P("shard", None, None),
        ),
        out_specs=(
            P(),
            P("shard", None, None),
            P("shard", None, None),
            P("shard", None, None),
            P(("dp", "shard")),
            P(("dp", "shard")),
            P(("dp", "shard")),
        ),
        check_vma=False,
    )
```

time: 809 us -> 405 us (0.50)
  blocking collectives: 345 us -> 0 us
  local copies, waits for them, and re-layouts: 186 us -> 112 us
  starting transfers between devices: 0.16 us -> 42.8 us
  Pallas kernels: 0 us -> 31.6 us
  matrix products: 103 us -> 81.5 us
  between operations: 16.6 us -> 3.12 us
  waiting for transfers between devices: 80.8 us -> 70.4 us
    psum x2 -> x0, blocking collectives: 345 us -> none  [the longest x1 306 us: body(): summed = lax.psum(grad_slot, 'dp')]
    concatenate x2 -> x7, local copies, waits for them, and re-layouts: 87.2 us -> 1.93 us  [the longest x2 0.76 us: gather_all(): second = jnp.concatenate([second, second_y])]
    all_gather x2 -> x0, waiting for transfers between devices: 80.8 us -> none  [the longest x1 54.4 us: body(): lax.all_gather(adam_flat.astype(jnp.bfloat16), ('dp', 'shard'), axis=0, t...]
    ppermute x0 -> x41, waiting for transfers between devices: none -> 70.4 us  [send(): return lax.ppermute(value, AXES, pairs)]
    ppermute x0 -> x41, starting transfers between devices: none -> 42.8 us  [send(): return lax.ppermute(value, AXES, pairs)]
    pallas_call x0 -> x5, Pallas kernels: none -> 31.6 us  [the longest x1 12 us: shampoo(): pl.pallas_call(functools.partial(shampoo_kernel, near), name='shampoo', g...]
    dot_general x43 -> x29, matrix products: 103 us -> 81.5 us  [the longest x20 64.8 us: mm(): return jnp.dot(left, right, preferred_element_type=F32)]
    reshape x19 -> x9, local copies, waits for them, and re-layouts: 34.6 us -> 19.5 us  [the longest x1 5.58 us: tokens(): projected = (matmul(act_one, w_qkv) + qkv_bias).astype(jnp.bfloat16).resh...]
  transfers between devices with their start and end apart: 4 -> 41, of which waited for: 2 -> 16; matrix products, arithmetic and copies ran while one was open for 7% -> 8% of each run, Pallas kernels for 0% -> 4%
where the time goes in v1:
time: 405 us; the launch traced here: 398 us
  local copies, waits for them, and re-layouts  112 us (28%)
  matrix products  81.5 us (20%)
  waiting for transfers between devices  70.4 us (17%)
  other arithmetic  57 us (14%)
  starting transfers between devices  42.8 us (11%)
  Pallas kernels  31.6 us (8%)
    ppermute x41, waiting for transfers between devices, send(): return lax.ppermute(value, AXES, pairs)  70.4 us
    dot_general x20, matrix products, mm(): return jnp.dot(left, right, preferred_element_type=F32)  64.8 us
    ppermute x41, starting transfers between devices, send(): return lax.ppermute(value, AXES, pairs)  42.8 us
    unnamed x325, local copies, waits for them, and re-layouts  22.8 us
    dot_general x4, local copies, waits for them, and re-layouts, mm(): return jnp.dot(left, right, preferred_element_type=F32)  12.7 us
    pallas_call x1, Pallas kernels, shampoo(): pl.pallas_call(functools.partial(shampoo_kernel, near), name='shampoo', g...  12 us
    convert_element_type x1, other arithmetic, tokens(): gelu_back(matmul(back_branch_two, w_down.T))[0].astype(jnp.bfloat16)  8.37 us
  transfers between devices with their start and end apart: 41, of which 16 were waited for; matrix products, arithmetic and copies ran while one was open for 8% of the time, Pallas kernels for 4%

profile of v1, /device:TPU:0, one launch (start us, length us, event | category | flops | bytes accessed | tf_op | source)
XLA Modules:
  0.0 398.1 jit_solution(4106703226520499411)
XLA Ops:
  23.2 5.4 %collective-permute-done.4 = bf16[4,256,128]{2,1,0:T(8,128)(2,1)S(1)} collective-permute-done((bf16[4,256,128]{2,1,0:T(8,128)(2,1)S(1)}, bf16[4,256,128]{2,1,0:T(8,128)(2,1)S(1)}, u32[]{:S(2)}, u32[]{:S(2)}) %collective-permute-start.4) | collective-permute-done | bytes 262176 | tf_op jit(solution)/shard_map/ppermute | solution.py:132
  35.2 17.4 %collective-permute-done.13.far_ref = bf16[3,192,384]{2,1,0:T(8,128)(2,1)} collective-permute-done((bf16[3,192,384]{2,1,0:T(8,128)(2,1)}, bf16[3,192,384]{2,1,0:T(8,128)(2,1)}, u32[]{:S(2)}, u32[]{:S(2)}) %collective-permute-start.13) | collective-permute-done | bytes 442400 | tf_op jit(solution)/shard_map/ppermute | solution.py:132
  59.5 4.1 %gather_blocks.1 = bf16[12,384,384]{2,1,0:T(8,128)(2,1)} custom-call(s32[4]{0:T(128)} %pad_add_fusion.at_ref.refs_0_, s32[12]{0:T(128)} %own_ref.1, bf16[3,384,384]{2,1,0:T(8,128)(2,1)} %copy-done.32, bf16[3,384,384]{2,1,0:T(8,128)(2,1)} %copy-done.52, bf16[3,192,384]{2,1,0:T(8,128)(2,1)} %collective-permute-done.12.near_ref, ...), custom_call_target="tpu_custom_call" | custom-call | bytes 7000000 | tf_op jit(solution)/shard_map/gather_blocks/pallas_call | solution.py:289
  68.8 5.6 %conditioning.1 = (f32[8,3072]{1,0:T(8,128)}, f32[8,384]{1,0:T(8,128)}, f32[8,384]{1,0:T(8,128)}, f32[8,384]{1,0:T(8,128)}, bf16[384,2304]{1,0:T(8,128)(2,1)}, /...) custom-call(s32[4]{0:T(128)} %pad_add_fusion.at_ref.refs_0_, ...), custom_call_target="tpu_custom_call" | custom-call | flops 1000000000 | bytes 10000000 | tf_op jit(solution)/shard_map/conditioning/pallas_call | solution.py:251
  93.1 4.5 %copy.109 = bf16[1024,1152]{0,1:T(8,128)(2,1)} copy(bf16[1024,1152]{1,0:T(8,128)(2,1)} %fusion.20) | data formatting | bytes 4718592 | tf_op jit(solution)/shard_map/convert_element_type | solution.py:622
  97.6 5.6 %reshape.457 = bf16[4,256,3,6,64]{1,0,4,3,2:T(4,128)(2,1)} reshape(bf16[1024,1152]{0,1:T(8,128)(2,1)} %copy.109) | data formatting | bytes 4718592 | tf_op jit(solution)/shard_map/reshape | solution.py:623
  114.2 3.6 fusion.117
  138.5 15.3 %fusion.116 = (f32[1024]{0:T(1024)S(1)}, f32[1024,384]{0,1:T(8,128)S(1)}, f32[1024,384]{0,1:T(8,128)}) fusion(f32[1024,384]{0,1:T(8,128)S(1)} %get-tuple-element.91, f32[1024,384]{0,1:T(8,128)S(1)} %copy-done.47, f32[384]{0:T(512)S(1)} %copy-done.128, bf16[1536,384]{1,0:T(8,128)(2,1)S(1)} %bitcast.395, f32[1024,1536]{1,0:T(8,128)S(1)} %fusion.59, ...), kind=kOutput, calls=%fused_computation.352 | convolution fusion | flops 1225260032 | bytes 13774336 | tf_op jit(solution)/shard_map/dot_general | solution.py:74
  163.3 3.1 copy.170
  168.3 3.6 copy.171
  182.7 7.9 %fusion.110 = (bf16[1536]{0:T(1024)(128)(2,1)}, bf16[1024,1536]{1,0:T(8,128)(2,1)S(1)}, f32[1024,1536]{1,0:T(8,128)}) fusion(f32[1024,1536]{1,0:T(8,128)S(1)} %bitcast.362, f32[1536]{0:T(1024)S(1)} %copy-done.107, bf16[1024,384]{1,0:T(8,128)(2,1)S(1)} %bitcast.403, bf16[1536,384]{1,0:T(8,128)(2,1)S(1)} %bitcast.396), kind=kOutput, calls=%fused_computation.347 | convolution fusion | flops 1242561024 | bytes 17703936 | tf_op jit(solution)/shard_map/dot_general | solution.py:74
  190.7 3.7 fusion.30
  194.4 3.2 copy.128
  202.5 3.9 multiply_reduce_fusion.2
  218.6 3.2 reshape.465
  221.8 5.0 %multiply_reduce_fusion = (f32[4,6,256]{2,1,0:T(8,128)S(1)}, f32[4,6,256,256]{2,3,1,0:T(8,128)S(1)}) fusion(f32[4,6,256,256]{2,3,1,0:T(8,128)} %copy-done, f32[4,6,256]{2,1,0:T(8,128)S(1)} %copy-done.54, bf16[4,256,1,6,64]{1,0,4,3,2:T(4,128)(2,1)S(1)} %copy-done.28, bf16[4,256,6,64]{1,0,3,2:T(4,128)(2,1)} %reshape.465), kind=kOutput, calls=%fused_computation.27 | convolution fusion | flops 207611904 | bytes 14204928 | tf_op jit(solution)/shard_map/gqhe,gkhe->ghqk/dot_general | solution.py:699
  236.3 3.5 copy.144
  253.3 3.3 fusion.33
  256.6 8.4 %fusion.13 = (bf16[1536,1024]{0,1:T(8,128)(2,1)}, bf16[1536,1024]{0,1:T(8,128)(2,1)}) fusion(f32[1024,1536]{1,0:T(8,128)} %get-tuple-element.146, f32[1024,1536]{1,0:T(8,128)S(1)} %bitcast.364, f32[1536]{0:T(1024)S(1)} %copy-done.108), kind=kLoop, calls=%fused_computation.18 | loop fusion | flops 36175872 | bytes 18880512 | tf_op jit(solution)/shard_map/convert_element_type | solution.py:678
  265.0 3.2 copy.168
  268.2 3.6 fusion.32
  271.7 4.8 %copy.169 = bf16[1536,1024]{1,0:T(8,128)(2,1)} copy(bf16[1536,1024]{0,1:T(8,128)(2,1)} %get-tuple-element.95) | data formatting | bytes 6291456 | tf_op jit(solution)/shard_map/dot_general | solution.py:74
  301.5 11.1 %collective-permute-done.19 = bf16[4,176,384]{2,1,0:T(8,128)(2,1)S(1)} collective-permute-done((bf16[4,176,384]{2,1,0:T(8,128)(2,1)S(1)}, bf16[4,176,384]{2,1,0:T(8,128)(2,1)S(1)}, u32[]{:S(2)}, u32[]{:S(2)}) %collective-permute-start.19) | collective-permute-done | bytes 540704 | tf_op jit(solution)/shard_map/ppermute | solution.py:132
  316.2 4.3 %collective-permute-done.20 = bf16[2,176,384]{2,1,0:T(8,128)(2,1)S(1)} collective-permute-done((bf16[2,176,384]{2,1,0:T(8,128)(2,1)S(1)}, bf16[2,176,384]{2,1,0:T(8,128)(2,1)S(1)}, u32[]{:S(2)}, u32[]{:S(2)}) %collective-permute-start.20) | collective-permute-done | bytes 270368 | tf_op jit(solution)/shard_map/ppermute | solution.py:132
  326.2 4.5 %collective-permute-done.21 = bf16[176,384]{1,0:T(8,128)(2,1)S(1)} collective-permute-done((bf16[176,384]{1,0:T(8,128)(2,1)S(1)}, bf16[176,384]{1,0:T(8,128)(2,1)S(1)}, u32[]{:S(2)}, u32[]{:S(2)}) %collective-permute-start.21) | collective-permute-done | bytes 135200 | tf_op jit(solution)/shard_map/ppermute | solution.py:132
  333.8 3.5 collective-permute-start.26
  339.7 3.8 collective-permute-done.25
  364.4 5.1 %collective-permute-done.29.refs_2_ = bf16[8,48,384]{2,1,0:T(8,128)(2,1)S(1)} collective-permute-done((bf16[8,48,384]{2,1,0:T(8,128)(2,1)S(1)}, bf16[8,48,384]{2,1,0:T(8,128)(2,1)S(1)}, u32[]{:S(2)}, u32[]{:S(2)}) %collective-permute-start.29) | collective-permute-done | bytes 294944 | tf_op jit(solution)/shard_map/ppermute | solution.py:132
  370.0 3.5 collective-permute-done.30.refs_3_
  374.3 12.0 %shampoo.1 = (f32[3,384,384]{2,1,0:T(8,128)}, f32[3,384,384]{2,1,0:T(8,128)}, f32[3,384,384]{2,1,0:T(8,128)}) custom-call(s32[4]{0:T(128)} %pad_add_fusion.at_ref.refs_0_, bf16[4,2,3,24,384]{4,3,2,1,0:T(8,128)(2,1)} %copy-done.60, bf16[4,2,3,24,384]{4,3,2,1,0:T(8,128)(2,1)} %copy-done.139, f32[3,384,384]{2,1,0:T(8,128)} %refs_2_.1, f32[3,384,384]{2,1,0:T(8,128)} %refs_3_.1, ...), custom_call_target="tpu_custom_call" | custom-call | flops 3000000000 | bytes 15000000 | tf_op jit(solution)/shard_map/shampoo/pallas_call | solution.py:538
  388.0 4.6 %place_gradients.1 = (f32[32,56,384]{2,1,0:T(8,128)}, f32[2,384,384]{2,1,0:T(8,128)}, f32[256,384]{1,0:T(8,128)}) custom-call(s32[4]{0:T(128)} %pad_add_fusion.at_ref.refs_0_, bf16[8,48,384]{2,1,0:T(8,128)(2,1)} %copy-done.63, bf16[8,40,384]{2,1,0:T(8,128)(2,1)} %copy-done.64, bf16[8,48,384]{2,1,0:T(8,128)(2,1)} %copy-done.73, ...), custom_call_target="tpu_custom_call" | custom-call | tf_op jit(solution)/shard_map/place_gradients/pallas_call | solution.py:463
  392.6 5.3 %adam.1 = (f32[1,1]{1,0:T(1,128)}, f32[520,128]{1,0:T(8,128)}, f32[520,128]{1,0:T(8,128)}, f32[520,128]{1,0:T(8,128)}) custom-call(f32[32,56,384]{2,1,0:T(8,128)} %get-tuple-element.39.pay_ref, f32[2,384,384]{2,1,0:T(8,128)} %get-tuple-element.40.align_ref, f32[256,384]{1,0:T(8,128)} %get-tuple-element.41.misc_ref, s32[4]{0:T(128)} %pad_add_fusion.at_ref.refs_0_, ...), custom_call_target="tpu_custom_call" | custom-call | flops 1000000000 | bytes 10000000 | tf_op jit(solution)/shard_map/adam/pallas_call | solution.py:471
  (606 shorter events, 215.6 us)
Async XLA Ops:
  1.6 14.5 %collective-permute-start = (bf16[520,128]{1,0:T(8,128)(2,1)S(1)}, bf16[520,128]{1,0:T(8,128)(2,1)S(1)}, u32[]{:S(2)}, u32[]{:S(2)}) collective-permute-start(bf16[520,128]{1,0:T(8,128)(2,1)S(1)} %bitcast_convert_fusion), channel_id=1, source_target_pairs={{0,8},{1,9},{2,10},{3,11},{4,12},{5,13},{6,14},{7,15},{8,16},{9,17... | collective-permute-start | bytes 399368 | tf_op jit(solution)/shard_map/ppermute | solution.py:132
  4.7 11.4 %collective-permute-start.1 = (bf16[520,128]{1,0:T(8,128)(2,1)S(1)}, bf16[520,128]{1,0:T(8,128)(2,1)S(1)}, u32[]{:S(2)}, u32[]{:S(2)}) collective-permute-start(bf16[520,128]{1,0:T(8,128)(2,1)S(1)} %bitcast_convert_fusion), channel_id=1, source_target_pairs={{0,16},{1,17},{2,18},{3,19},{4,20},{5,21},{6,22},{7,23},{8,24},{9,... | collective-permute-start | bytes 399368 | tf_op jit(solution)/shard_map/ppermute | solution.py:132
  7.3 8.3 %collective-permute-start.2 = (bf16[520,128]{1,0:T(8,128)(2,1)S(1)}, bf16[520,128]{1,0:T(8,128)(2,1)S(1)}, u32[]{:S(2)}, u32[]{:S(2)}) collective-permute-start(bf16[520,128]{1,0:T(8,128)(2,1)S(1)} %bitcast_convert_fusion), channel_id=1, source_target_pairs={{0,24},{1,25},{2,26},{3,27},{4,28},{5,29},{6,30},{7,31},{8,0},{9,1... | collective-permute-start | bytes 399368 | tf_op jit(solution)/shard_map/ppermute | solution.py:132
  10.3 43.5 %collective-permute-start.11 = (bf16[3,384,384]{2,1,0:T(8,128)(2,1)S(1)}, bf16[3,384,384]{2,1,0:T(8,128)(2,1)S(1)}, u32[]{:S(2)}, u32[]{:S(2)}) collective-permute-start(bf16[3,384,384]{2,1,0:T(8,128)(2,1)S(1)} %convert_element_type.351.mine_ref), channel_id=1, source_target_pairs={{0,1},{1,0},{2,3},{3,2},{4,5},{5,4},{6,7},{7,6},{8,9},{9,8},{10,11... | collective-permute-start | bytes 2654216 | tf_op jit(solution)/shard_map/ppermute | solution.py:132
  10.4 22.7 %collective-permute-start.12 = (bf16[3,192,384]{2,1,0:T(8,128)(2,1)S(1)}, bf16[3,192,384]{2,1,0:T(8,128)(2,1)}, u32[]{:S(2)}, u32[]{:S(2)}) collective-permute-start(bf16[3,192,384]{2,1,0:T(8,128)(2,1)S(1)} %constant_dynamic-slice_fusion.4), channel_id=1, source_target_pairs={{0,2},{1,3},{2,0},{3,1},{4,6},{5,7},{6,4},{7,5},{8,10},{9,11},{10,... | collective-permute-start | bytes 1327112 | tf_op jit(solution)/shard_map/ppermute | solution.py:132
  16.2 12.5 %collective-permute-start.4 = (bf16[4,256,128]{2,1,0:T(8,128)(2,1)S(1)}, bf16[4,256,128]{2,1,0:T(8,128)(2,1)S(1)}, u32[]{:S(2)}, u32[]{:S(2)}) collective-permute-start(bf16[4,256,128]{2,1,0:T(8,128)(2,1)S(1)} %pad_maximum_fusion.9), channel_id=1, source_target_pairs={{0,2},{1,3},{2,0},{3,1},{4,6},{5,7},{6,4},{7,5},{8,10},{9,11},{10,... | collective-permute-start | bytes 786440 | tf_op jit(solution)/shard_map/ppermute | solution.py:132
  17.9 13.0 %collective-permute-start.3 = (bf16[4,264,128]{2,1,0:T(8,128)(2,1)S(1)}, bf16[4,264,128]{2,1,0:T(8,128)(2,1)S(1)}, u32[]{:S(2)}, u32[]{:S(2)}) collective-permute-start(bf16[4,264,128]{2,1,0:T(8,128)(2,1)S(1)} %pad_maximum_fusion.8), channel_id=1, source_target_pairs={{0,4},{1,5},{2,6},{3,7},{4,0},{5,1},{6,2},{7,3},{8,12},{9,13},{10,... | collective-permute-start | bytes 811016 | tf_op jit(solution)/shard_map/ppermute | solution.py:132
  29.4 24.4 %collective-permute-start.6 = (bf16[8,256,128]{2,1,0:T(8,128)(2,1)}, bf16[8,256,128]{2,1,0:T(8,128)(2,1)}, u32[]{:S(2)}, u32[]{:S(2)}) collective-permute-start(bf16[8,256,128]{2,1,0:T(8,128)(2,1)} %constant_dynamic-update-slice_fusion.5.refs_1_), channel_id=1, source_target_pairs={{0,4},{1,5},{2,6},{3,7},{4,0},{5,1},{6,2},{7,3},{8,12},{9,13},{10,... | collective-permute-start | bytes 1572872 | tf_op jit(solution)/shard_map/ppermute | solution.py:132
  31.6 22.6 %collective-permute-start.5 = (bf16[8,264,128]{2,1,0:T(8,128)(2,1)}, bf16[8,264,128]{2,1,0:T(8,128)(2,1)}, u32[]{:S(2)}, u32[]{:S(2)}) collective-permute-start(bf16[8,264,128]{2,1,0:T(8,128)(2,1)} %constant_dynamic-update-slice_fusion.refs_0_), channel_id=1, source_target_pairs={{0,2},{1,3},{2,0},{3,1},{4,6},{5,7},{6,4},{7,5},{8,10},{9,11},{10,... | collective-permute-start | bytes 1622024 | tf_op jit(solution)/shard_map/ppermute | solution.py:132
  33.1 19.5 %collective-permute-start.13 = (bf16[3,192,384]{2,1,0:T(8,128)(2,1)}, bf16[3,192,384]{2,1,0:T(8,128)(2,1)}, u32[]{:S(2)}, u32[]{:S(2)}) collective-permute-start(bf16[3,192,384]{2,1,0:T(8,128)(2,1)} %collective-permute-done.12.near_ref), channel_id=1, source_target_pairs={{0,4},{1,5},{2,6},{3,7},{4,0},{5,1},{6,2},{7,3},{8,12},{9,13},{10,... | collective-permute-start | bytes 1327112 | tf_op jit(solution)/shard_map/ppermute | solution.py:132
  33.9 19.3 %collective-permute-start.14 = (bf16[3,192,384]{2,1,0:T(8,128)(2,1)}, bf16[3,192,384]{2,1,0:T(8,128)(2,1)S(1)}, u32[]{:S(2)}, u32[]{:S(2)}) collective-permute-start(bf16[3,192,384]{2,1,0:T(8,128)(2,1)} %collective-permute-done.12.near_ref), channel_id=1, source_target_pairs={{0,1},{1,0},{2,3},{3,2},{4,5},{5,4},{6,7},{7,6},{8,9},{9,8},{10,11... | collective-permute-start | bytes 1327112 | tf_op jit(solution)/shard_map/ppermute | solution.py:132
  53.2 15.6 %collective-permute-start.8 = (bf16[8,256,128]{2,1,0:T(8,128)(2,1)}, bf16[8,256,128]{2,1,0:T(8,128)(2,1)}, u32[]{:S(2)}, u32[]{:S(2)}) collective-permute-start(bf16[8,256,128]{2,1,0:T(8,128)(2,1)} %constant_dynamic-update-slice_fusion.5.refs_1_), channel_id=1, source_target_pairs={{0,1},{1,0},{2,3},{3,2},{4,5},{5,4},{6,7},{7,6},{8,9},{9,8},{10,11... | collective-permute-start | bytes 1572872 | tf_op jit(solution)/shard_map/ppermute | solution.py:132
  53.7 15.1 %collective-permute-start.7 = (bf16[8,264,128]{2,1,0:T(8,128)(2,1)}, bf16[8,264,128]{2,1,0:T(8,128)(2,1)}, u32[]{:S(2)}, u32[]{:S(2)}) collective-permute-start(bf16[8,264,128]{2,1,0:T(8,128)(2,1)} %constant_dynamic-update-slice_fusion.refs_0_), channel_id=1, source_target_pairs={{0,1},{1,0},{2,3},{3,2},{4,5},{5,4},{6,7},{7,6},{8,9},{9,8},{10,11... | collective-permute-start | bytes 1622024 | tf_op jit(solution)/shard_map/ppermute | solution.py:132
  53.8 15.0 %collective-permute-start.10 = (bf16[8,256,128]{2,1,0:T(8,128)(2,1)}, bf16[8,256,128]{2,1,0:T(8,128)(2,1)}, u32[]{:S(2)}, u32[]{:S(2)}) collective-permute-start(bf16[8,256,128]{2,1,0:T(8,128)(2,1)} %collective-permute-done.6.refs_3_), channel_id=1, source_target_pairs={{0,1},{1,0},{2,3},{3,2},{4,5},{5,4},{6,7},{7,6},{8,9},{9,8},{10,11... | collective-permute-start | bytes 1572872 | tf_op jit(solution)/shard_map/ppermute | solution.py:132
  54.3 14.6 %collective-permute-start.9 = (bf16[8,264,128]{2,1,0:T(8,128)(2,1)}, bf16[8,264,128]{2,1,0:T(8,128)(2,1)}, u32[]{:S(2)}, u32[]{:S(2)}) collective-permute-start(bf16[8,264,128]{2,1,0:T(8,128)(2,1)} %collective-permute-done.5.refs_2_), channel_id=1, source_target_pairs={{0,1},{1,0},{2,3},{3,2},{4,5},{5,4},{6,7},{7,6},{8,9},{9,8},{10,11... | collective-permute-start | bytes 1622024 | tf_op jit(solution)/shard_map/ppermute | solution.py:132
  298.3 14.3 %collective-permute-start.19 = (bf16[4,176,384]{2,1,0:T(8,128)(2,1)S(1)}, bf16[4,176,384]{2,1,0:T(8,128)(2,1)S(1)}, u32[]{:S(2)}, u32[]{:S(2)}) collective-permute-start(bf16[4,176,384]{2,1,0:T(8,128)(2,1)S(1)} %constant_dynamic-slice_fusion.1), channel_id=1, source_target_pairs={{0,2},{1,3},{2,0},{3,1},{4,6},{5,7},{6,4},{7,5},{8,10},{9,11},{10,... | collective-permute-start | bytes 1622024 | tf_op jit(solution)/shard_map/ppermute | solution.py:132
  299.9 14.4 %collective-permute-start.17 = (bf16[4,176,384]{2,1,0:T(8,128)(2,1)S(1)}, bf16[4,176,384]{2,1,0:T(8,128)(2,1)S(1)}, u32[]{:S(2)}, u32[]{:S(2)}) collective-permute-start(bf16[4,176,384]{2,1,0:T(8,128)(2,1)S(1)} %constant_dynamic-slice_fusion.3), channel_id=1, source_target_pairs={{0,4},{1,5},{2,6},{3,7},{4,0},{5,1},{6,2},{7,3},{8,12},{9,13},{10,... | collective-permute-start | bytes 1622024 | tf_op jit(solution)/shard_map/ppermute | solution.py:132
  312.8 7.7 %collective-permute-start.20 = (bf16[2,176,384]{2,1,0:T(8,128)(2,1)S(1)}, bf16[2,176,384]{2,1,0:T(8,128)(2,1)S(1)}, u32[]{:S(2)}, u32[]{:S(2)}) collective-permute-start(bf16[2,176,384]{2,1,0:T(8,128)(2,1)S(1)} %constant_dynamic-slice_fusion), channel_id=1, source_target_pairs={{0,4},{1,5},{2,6},{3,7},{4,0},{5,1},{6,2},{7,3},{8,12},{9,13},{10,... | collective-permute-start | bytes 811016 | tf_op jit(solution)/shard_map/ppermute | solution.py:132
  314.6 7.4 %collective-permute-start.18 = (bf16[2,176,384]{2,1,0:T(8,128)(2,1)S(1)}, bf16[2,176,384]{2,1,0:T(8,128)(2,1)S(1)}, u32[]{:S(2)}, u32[]{:S(2)}) collective-permute-start(bf16[2,176,384]{2,1,0:T(8,128)(2,1)S(1)} %constant_dynamic-slice_fusion.2), channel_id=1, source_target_pairs={{0,2},{1,3},{2,0},{3,1},{4,6},{5,7},{6,4},{7,5},{8,10},{9,11},{10,... | collective-permute-start | bytes 811016 | tf_op jit(solution)/shard_map/ppermute | solution.py:132
  322.3 8.4 %collective-permute-start.21 = (bf16[176,384]{1,0:T(8,128)(2,1)S(1)}, bf16[176,384]{1,0:T(8,128)(2,1)S(1)}, u32[]{:S(2)}, u32[]{:S(2)}) collective-permute-start(bf16[176,384]{1,0:T(8,128)(2,1)S(1)} %get-tuple-element.108), channel_id=1, source_target_pairs={{0,8},{1,9},{2,10},{3,11},{4,12},{5,13},{6,14},{7,15},{8,16},{9,17... | collective-permute-start | bytes 405512 | tf_op jit(solution)/shard_map/ppermute | solution.py:132
  323.0 10.6 %collective-permute-start.22 = (bf16[176,384]{1,0:T(8,128)(2,1)S(1)}, bf16[176,384]{1,0:T(8,128)(2,1)S(1)}, u32[]{:S(2)}, u32[]{:S(2)}) collective-permute-start(bf16[176,384]{1,0:T(8,128)(2,1)S(1)} %get-tuple-element.109), channel_id=1, source_target_pairs={{0,16},{1,17},{2,18},{3,19},{4,20},{5,21},{6,22},{7,23},{8,24},{9,... | collective-permute-start | bytes 405512 | tf_op jit(solution)/shard_map/ppermute | solution.py:132
  323.1 10.5 %collective-permute-start.23 = (bf16[176,384]{1,0:T(8,128)(2,1)S(1)}, bf16[176,384]{1,0:T(8,128)(2,1)S(1)}, u32[]{:S(2)}, u32[]{:S(2)}) collective-permute-start(bf16[176,384]{1,0:T(8,128)(2,1)S(1)} %get-tuple-element.110), channel_id=1, source_target_pairs={{0,24},{1,25},{2,26},{3,27},{4,28},{5,29},{6,30},{7,31},{8,0},{9,1... | collective-permute-start | bytes 405512 | tf_op jit(solution)/shard_map/ppermute | solution.py:132
  338.2 8.5 %collective-permute-start.35 = (bf16[6,24,384]{2,1,0:T(8,128)(2,1)S(1)}, bf16[6,24,384]{2,1,0:T(8,128)(2,1)S(1)}, u32[]{:S(2)}, u32[]{:S(2)}) collective-permute-start(bf16[6,24,384]{2,1,0:T(8,128)(2,1)S(1)} %bitcast.408), channel_id=1, source_target_pairs={{0,1},{1,0},{2,3},{3,2},{4,5},{5,4},{6,7},{7,6},{8,9},{9,8},{10,11... | collective-permute-start | bytes 331784 | tf_op jit(solution)/shard_map/ppermute | solution.py:132
  344.3 18.9 %collective-permute-start.28 = (bf16[4,40,384]{2,1,0:T(8,128)(2,1)S(1)}, bf16[4,40,384]{2,1,0:T(8,128)(2,1)S(1)}, u32[]{:S(2)}, u32[]{:S(2)}) collective-permute-start(bf16[4,40,384]{2,1,0:T(8,128)(2,1)S(1)} %pad_maximum_fusion.13), channel_id=1, source_target_pairs={{0,2},{1,3},{2,0},{3,1},{4,6},{5,7},{6,4},{7,5},{8,10},{9,11},{10,... | collective-permute-start | bytes 368648 | tf_op jit(solution)/shard_map/ppermute | solution.py:132
  346.0 16.7 %collective-permute-start.27 = (bf16[4,48,384]{2,1,0:T(8,128)(2,1)S(1)}, bf16[4,48,384]{2,1,0:T(8,128)(2,1)S(1)}, u32[]{:S(2)}, u32[]{:S(2)}) collective-permute-start(bf16[4,48,384]{2,1,0:T(8,128)(2,1)S(1)} %pad_maximum_fusion.12), channel_id=1, source_target_pairs={{0,4},{1,5},{2,6},{3,7},{4,0},{5,1},{6,2},{7,3},{8,12},{9,13},{10,... | collective-permute-start | bytes 442376 | tf_op jit(solution)/shard_map/ppermute | solution.py:132
  351.9 9.0 %collective-permute-start.38 = (bf16[2,3,24,384]{3,2,1,0:T(8,128)(2,1)S(1)}, bf16[2,3,24,384]{3,2,1,0:T(8,128)(2,1)S(1)}, u32[]{:S(2)}, u32[]{:S(2)}) collective-permute-start(bf16[2,3,24,384]{3,2,1,0:T(8,128)(2,1)S(1)} %get-tuple-element.114), channel_id=1, source_target_pairs={{0,16},{1,17},{2,18},{3,19},{4,20},{5,21},{6,22},{7,23},{8,24},{9,... | collective-permute-start | bytes 331784 | tf_op jit(solution)/shard_map/ppermute | solution.py:132
  361.0 12.5 %collective-permute-start.40 = (bf16[4,2,3,24,384]{4,3,2,1,0:T(8,128)(2,1)S(1)}, bf16[4,2,3,24,384]{4,3,2,1,0:T(8,128)(2,1)S(1)}, u32[]{:S(2)}, u32[]{:S(2)}) collective-permute-start(bf16[4,2,3,24,384]{4,3,2,1,0:T(8,128)(2,1)S(1)} %pad_maximum_fusion.4.refs_0_), channel_id=1, source_target_pairs={{0,4},{1,5},{2,6},{3,7},{4,0},{5,1},{6,2},{7,3},{8,12},{9,13},{10,... | collective-permute-start | bytes 1327112 | tf_op jit(solution)/shard_map/ppermute | solution.py:132
  363.3 10.2 %collective-permute-start.30 = (bf16[8,40,384]{2,1,0:T(8,128)(2,1)S(1)}, bf16[8,40,384]{2,1,0:T(8,128)(2,1)S(1)}, u32[]{:S(2)}, u32[]{:S(2)}) collective-permute-start(bf16[8,40,384]{2,1,0:T(8,128)(2,1)S(1)} %constant_dynamic-update-slice_fusion.36.refs_1_), channel_id=1, source_target_pairs={{0,4},{1,5},{2,6},{3,7},{4,0},{5,1},{6,2},{7,3},{8,12},{9,13},{10,... | collective-permute-start | bytes 737288 | tf_op jit(solution)/shard_map/ppermute | solution.py:132
  364.4 22.0 %collective-permute-start.31 = (bf16[8,48,384]{2,1,0:T(8,128)(2,1)S(1)}, bf16[8,48,384]{2,1,0:T(8,128)(2,1)S(1)}, u32[]{:S(2)}, u32[]{:S(2)}) collective-permute-start(bf16[8,48,384]{2,1,0:T(8,128)(2,1)S(1)} %constant_dynamic-update-slice_fusion.31.refs_0_), channel_id=1, source_target_pairs={{0,1},{1,0},{2,3},{3,2},{4,5},{5,4},{6,7},{7,6},{8,9},{9,8},{10,11... | collective-permute-start | bytes 884744 | tf_op jit(solution)/shard_map/ppermute | solution.py:132
  369.5 16.9 %collective-permute-start.33 = (bf16[8,48,384]{2,1,0:T(8,128)(2,1)S(1)}, bf16[8,48,384]{2,1,0:T(8,128)(2,1)S(1)}, u32[]{:S(2)}, u32[]{:S(2)}) collective-permute-start(bf16[8,48,384]{2,1,0:T(8,128)(2,1)S(1)} %collective-permute-done.29.refs_2_), channel_id=1, source_target_pairs={{0,1},{1,0},{2,3},{3,2},{4,5},{5,4},{6,7},{7,6},{8,9},{9,8},{10,11... | collective-permute-start | bytes 884744 | tf_op jit(solution)/shard_map/ppermute | solution.py:132
  369.5 16.9 %collective-permute-start.32 = (bf16[8,40,384]{2,1,0:T(8,128)(2,1)S(1)}, bf16[8,40,384]{2,1,0:T(8,128)(2,1)S(1)}, u32[]{:S(2)}, u32[]{:S(2)}) collective-permute-start(bf16[8,40,384]{2,1,0:T(8,128)(2,1)S(1)} %constant_dynamic-update-slice_fusion.36.refs_1_), channel_id=1, source_target_pairs={{0,1},{1,0},{2,3},{3,2},{4,5},{5,4},{6,7},{7,6},{8,9},{9,8},{10,11... | collective-permute-start | bytes 737288 | tf_op jit(solution)/shard_map/ppermute | solution.py:132
  373.5 12.9 %collective-permute-start.34 = (bf16[8,40,384]{2,1,0:T(8,128)(2,1)S(1)}, bf16[8,40,384]{2,1,0:T(8,128)(2,1)S(1)}, u32[]{:S(2)}, u32[]{:S(2)}) collective-permute-start(bf16[8,40,384]{2,1,0:T(8,128)(2,1)S(1)} %collective-permute-done.30.refs_3_), channel_id=1, source_target_pairs={{0,1},{1,0},{2,3},{3,2},{4,5},{5,4},{6,7},{7,6},{8,9},{9,8},{10,11... | collective-permute-start | bytes 737288 | tf_op jit(solution)/shard_map/ppermute | solution.py:132
  (158 other events, 738.2 us)
